TPU v7x, 256 devices: a whole 4x4x8 slice. The times are simulated.
256 devices in a mesh: grp: 2 (over y_lo), dp: 8 (over x, core), mp: 16 (over y_hi, z).
Axes of the slice: x: 4, y: 4 (y_hi: 2, y_lo: 2; y = y_hi * 2 + y_lo), z: 8, core: 2. Of those that a mesh axis runs over, the one named last changes fastest.
Arguments:
- teacher_hidden: bfloat16 [32768, 8192], P('dp', 'mp'), may hold values from -6 to 6
- teacher_gain: bfloat16 [8192], P('mp'), may hold values from 0.25 to 1.75
- teacher_value: bfloat16 [8192, 1024], P('mp', 'grp'), may hold values from -0.0625 to 0.0625
- student_hidden: bfloat16 [32768, 4096], P(('dp', 'mp')), may hold values from -24 to 24
- student_gain: bfloat16 [4096], replicated, may hold values from 0.25 to 1.75
- student_value: bfloat16 [4096, 1024], P(('dp', 'mp'), 'grp'), may hold values from -0.09375 to 0.09375
- segment_ids: int32 [32, 1024], P('dp'), may hold values from 0 to 7, never falling along the last dimension, each value on 1 to 384 neighbouring positions
Outputs:
- value_grad: float32 [4096, 1024], P(('dp', 'mp'), 'grp')
Inputs may be any that keep to these rules, and one draw needn't show every extreme that they name: `segment_ids`: in every row the ids never fall; each id from 0 to 7 covers 1 to 384 consecutive positions, and one covers exactly 384.
All inputs are finite; a program needn't handle non-finite values.
Results may differ from a plain program's by a relative error of at most 0.0031.
Values may be sent and summed in bfloat16 or wider, within the bound.
A program may use at most 64 MiB of HBM per device.

v0:
```python
import jax
import jax.numpy as jnp
from jax import lax
from jax.sharding import PartitionSpec as P

DT = 8192
KV = 1024
NSEG = 8


norm_eps = 1e-05
power_eps = 1e-06


def per_device(
    teacher_hidden,
    teacher_gain,
    teacher_value,
    student_hidden,
    student_gain,
    student_value,
    segment_ids,
):
    tok_dev = student_hidden.shape[0]
    member = lax.axis_index("mp")
    teacher_wide = teacher_hidden.astype(jnp.float32)
    scaled = (teacher_wide * teacher_gain.astype(jnp.float32)).astype(jnp.bfloat16)
    row_block = scaled
    projected = lax.psum_scatter(
        jnp.dot(row_block, teacher_value, preferred_element_type=jnp.float32),
        "mp",
        scatter_dimension=0,
        tiled=True,
    )
    squares = lax.psum_scatter(
        jnp.sum(teacher_wide * teacher_wide, axis=1), "mp", scatter_dimension=0, tiled=True
    )
    teacher_scale = lax.rsqrt(squares / DT + norm_eps)
    target = projected * teacher_scale[:, None]
    power_half = jnp.sum(target * target, axis=1)
    target_power = lax.psum(power_half, "grp") / KV + power_eps
    student_wide = student_hidden.astype(jnp.float32)
    student_scale = lax.rsqrt(
        jnp.mean(student_wide * student_wide, axis=1, keepdims=True) + norm_eps
    )
    normed = (student_wide * student_scale * student_gain.astype(jnp.float32)).astype(jnp.bfloat16)
    states = jnp.dot(
        normed,
        lax.all_gather(student_value, ("dp", "mp"), axis=0, tiled=True),
        preferred_element_type=jnp.float32,
    )
    matches = segment_ids[:, :, None] == jnp.arange(NSEG, dtype=jnp.int32)[None, None, :]
    counts = jnp.sum(matches.astype(jnp.int32), axis=1)
    lengths = jnp.sum(jnp.where(matches, counts[:, None, :], 0), axis=2).reshape(-1)
    doc_length = lax.dynamic_slice_in_dim(lengths, member * tok_dev, tok_dev, 0).astype(jnp.float32)
    weighted = ((states - target) / (doc_length * target_power)[:, None]).astype(jnp.bfloat16)
    row_block = normed
    return lax.psum_scatter(
        lax.dot_general(
            row_block, weighted, (((0,), (0,)), ((), ())), preferred_element_type=jnp.float32
        ),
        ("dp", "mp"),
        scatter_dimension=0,
        tiled=True,
    )


def solution(mesh):
    return jax.shard_map(
        per_device,
        mesh=mesh,
        in_specs=(
            P("dp", "mp"),
            P("mp"),
            P("mp", "grp"),
            P(("dp", "mp"), None),
            P(),
            P(("dp", "mp"), "grp"),
            P("dp", None),
        ),
        out_specs=P(("dp", "mp"), "grp"),
        check_vma=False,
    )
```

profile of v0, /device:TPU:8, one launch (start us, length us, event | category | flops | bytes accessed | tf_op | source)
XLA Modules:
  0.0 944.8 jit_solution(1745123690488058740)
XLA Ops:
  7.4 0.0 copy-start
  7.4 0.0 reduce-scatter.3.cloned.1.call-start
  7.4 0.7 convert_element_type.31
  8.1 0.3 copy-done
  8.4 7.8 fusion.5
  16.2 0.0 copy-start.4
  16.2 0.0 copy-start.2
  16.2 0.0 copy-start.3
  16.2 0.0 reduce-scatter.3.cloned.1.call-update
  16.2 0.0 copy-start.1
  16.2 0.0 all-gather.2.cloned.1.call-start
  16.3 0.5 all-gather.2.cloned.1.call-update
  16.8 0.0 reduce-scatter.5.cloned.1.call-start
  16.9 0.0 copy-done.4
  16.9 0.6 dynamic-slice
  18.1 0.0 copy-done.2
  18.1 0.2 convert_reduce_fusion
  18.3 0.1 select_reduce_fusion
  18.4 0.0 copy-done.3
  18.4 3.1 fusion.1
  21.5 79.8 %all-reduce = f32[4096]{0:T(1024)S(1)} all-reduce(f32[4096]{0:T(1024)S(1)} %fusion.1), channel_id=3, replica_groups=mesh['grp'=2,'dp'=8,'mp'=16] {'mp'}, use_global_device_ids=true, to_apply=%region_3.0.clone | all-reduce | flops 4096 | bytes 32768
  101.3 0.1 fusion.17
  101.4 0.0 copy-done.1
  101.4 0.5 fusion.2
  101.9 142.2 %reduce-scatter.3.cloned.1.call-done = f32[256,512]{1,0:T(8,128)} async-done(((f32[4096,512]{1,0:T(8,128)}), f32[256,512]{1,0:T(8,128)}) %reduce-scatter.3.cloned.1.call-update) | async-done | bytes 524304 | tf_op jit(solution)/shard_map/reduce_scatter | solution.py:29
  244.1 1.2 multiply_reduce_fusion
  245.3 4.9 psum.7
  250.3 0.1 add_multiply_fusion
  250.3 0.0 all-gather.2.cloned.1.call-done
  250.3 8.1 fusion.10
  258.4 0.0 reduce-scatter.5.cloned.1.call-update
  258.4 678.9 %reduce-scatter.5.cloned.1.call-done = f32[32,512]{1,0:T(8,128)} async-done(((f32[4096,512]{1,0:T(8,128)}), f32[32,512]{1,0:T(8,128)}) %reduce-scatter.5.cloned.1.call-update) | async-done | bytes 65552 | tf_op jit(solution)/shard_map/reduce_scatter | solution.py:58
  (3 shorter events, 0.0 us)
Async XLA Ops:
  7.4 1.1 copy-start
  7.4 236.7 %reduce-scatter.3.cloned.1.call-start = ((), (), s32[]{:S(2)}) async-start(), calls=%async_computation.3 | async-start | bytes 8912896 | tf_op jit(solution)/shard_map/reduce_scatter | solution.py:29
  16.2 0.7 copy-start.4
  16.2 1.9 copy-start.2
  16.2 2.2 copy-start.3
  16.2 85.1 %copy-start.1 = (bf16[256,4096]{1,0:T(8,128)(2,1)S(1)}, bf16[256,4096]{1,0:T(8,128)(2,1)}, u32[]{:S(2)}) copy-start(bf16[256,4096]{1,0:T(8,128)(2,1)} %param.10) | copy-start | bytes 6291460
  16.2 234.1 %all-gather.2.cloned.1.call-start = ((), (), s32[]{:S(2)}) async-start(), calls=%async_computation.2 | async-start | bytes 4227072 | tf_op jit(solution)/shard_map/all_gather | solution.py:49
  16.8 920.6 %reduce-scatter.5.cloned.1.call-start = ((), (), s32[]{:S(2)}) async-start(), calls=%async_computation.4 | async-start | bytes 8454144 | tf_op jit(solution)/shard_map/reduce_scatter | solution.py:58
Sparse Core Ops, SparseCore 0:
  16.3 227.6 reduce-scatter.2
Sparse Core Ops, SparseCore 1:
  20.6 125.8 all-gather.1
  258.5 678.8 reduce-scatter.4
where the time goes:
time: 945 us
  waiting for transfers between devices  822 us (87%)
  blocking collectives  84.7 us (9%)
  matrix products  15.8 us (2%)
  between operations  15.6 us (2%)
    reduce_scatter x1, waiting for transfers between devices, per_device(): lax.psum_scatter(lax.dot_general(row_block, weighted, (((0,), (0,)), ((),...  679 us
    reduce_scatter x1, waiting for transfers between devices, per_device(): lax.psum_scatter(jnp.dot(row_block, teacher_value, preferred_element_type...  142 us
    unnamed x1, blocking collectives  79.8 us
  transfers between devices with their start and end apart: 3, of which 2 were waited for; matrix products, arithmetic and copies ran while one was open for 1% of the time, Pallas kernels for 0%

commit v1 on v0

v1 whole, which is shorter than its diff:
```python
import jax
import jax.numpy as jnp
from jax import lax
from jax.experimental import pallas as pl
from jax.experimental.pallas import tpu as pltpu
from jax.sharding import PartitionSpec as P

DT = 8192
DS = 4096
KV = 1024
NSEG = 8
MESH = pl.DeviceIdType.MESH
F32 = jnp.float32
BF16 = jnp.bfloat16

norm_eps = 1e-05
power_eps = 1e-06

ORDER = (4, 3, -3, 2, -2, 1, -1, 0)


def kernel(
    hid_ref,
    gain_ref,
    val_ref,
    stu_ref,
    sgain_ref,
    wsh_ref,
    seg_ref,
    out_ref,
    own,
    oth,
    valo,
    gaino,
    nrm,
    nall,
    wgt,
    ring_s,
    ring_r,
    sq_s,
    sq_r,
    states,
    total,
    pow_s,
    pow_r,
    len_row,
    wall,
    grad,
    grad_s,
    grad_r,
    loc_sem,
    hid_ss,
    hid_rs,
    fwd_ss,
    fwd_rs,
    misc_ss,
    misc_rs,
    wz_ss,
    wz_rs,
    wx_ss,
    wx_rs,
    wc_ss,
    wc_rs,
    nrm_ss,
    nrm_rs,
    ring_ss,
    ring_rs,
    sq_ss,
    sq_rs,
    wal_ss,
    wal_rs,
    wac_ss,
    wac_rs,
    grad_ss,
    grad_rs,
):
    g = lax.axis_index("grp")
    dp = lax.axis_index("dp")
    mp = lax.axis_index("mp")
    x, c = dp // 2, dp % 2
    h, z = mp // 8, mp % 8

    def at(grp=None, xx=None, cc=None, hh=None, zz=None):
        return (
            g if grp is None else grp,
            (x if xx is None else xx) * 2 + (c if cc is None else cc),
            (h if hh is None else hh) * 8 + (z if zz is None else zz),
        )

    def rc(src, dst, ss, rs, dev):
        return pltpu.make_async_remote_copy(
            src_ref=src, dst_ref=dst, send_sem=ss, recv_sem=rs, device_id=dev, device_id_type=MESH
        )

    zp = lambda d: lax.rem(z + d + 8, 8)
    xp = lambda e: lax.rem(x + e + 4, 4)
    grp_dev = at(grp=1 - g)
    cross_dev = at(grp=1 - g, hh=1 - h)
    far_dev = at(hh=1 - h)
    core_dev = at(cc=1 - c)

    own_cp = pltpu.make_async_copy(
        hid_ref.at[pl.ds(pl.multiple_of(h * 2048, 2048), 2048), :], own, loc_sem.at[0]
    )
    own_cp.start()
    w_cp = pltpu.make_async_copy(
        wsh_ref, wgt.at[dp, h, pl.ds(pl.multiple_of(z * 32, 32), 32), :], loc_sem.at[1]
    )
    w_cp.start()

    barrier = pltpu.get_barrier_semaphore()
    count = 0
    for d in range(1, 8):
        pl.semaphore_signal(barrier, inc=1, device_id=at(zz=zp(d)), device_id_type=MESH)
        count += 1
    for d in range(8):
        pl.semaphore_signal(barrier, inc=1, device_id=at(hh=1 - h, zz=zp(d)), device_id_type=MESH)
        count += 1
    for e in range(1, 4):
        for cc in range(2):
            pl.semaphore_signal(
                barrier, inc=1, device_id=at(xx=xp(e), cc=cc), device_id_type=MESH
            )
            count += 1
    for dev in (grp_dev, cross_dev, core_dev):
        pl.semaphore_signal(barrier, inc=1, device_id=dev, device_id_type=MESH)
        count += 1
    pl.semaphore_wait(barrier, count)

    half = pl.ds(pl.multiple_of(c * 256, 256), 256)
    half_o = pl.ds(pl.multiple_of((1 - c) * 256, 256), 256)
    val_cp = rc(val_ref.at[half, :], valo.at[half, :], misc_ss.at[0], misc_rs.at[0], far_dev)
    val_cp.start()
    val_fw = rc(valo.at[half, :], valo.at[half, :], misc_ss.at[1], misc_rs.at[1], core_dev)
    val_in = rc(valo.at[half_o, :], valo.at[half_o, :], misc_ss.at[1], misc_rs.at[1], core_dev)
    gain_cp = rc(gain_ref, gaino, misc_ss.at[2], misc_rs.at[2], cross_dev)
    gain_cp.start()
    wrow = lambda hh: wgt.at[dp, hh, pl.ds(pl.multiple_of(z * 32, 32), 32), :]
    w_far = rc(wsh_ref, wrow(h), misc_ss.at[3], misc_rs.at[3], far_dev)
    w_far_in = rc(wsh_ref, wrow(1 - h), misc_ss.at[3], misc_rs.at[3], far_dev)
    w_far.start()

    def hid_rows(hh, i, j):
        return pl.ds(pl.multiple_of(hh * 2048 + zp(ORDER[i]) * 256 + j * 128, 128), 128)

    def loc_rows(i, j):
        return pl.ds(pl.multiple_of(zp(ORDER[i]) * 256 + j * 128, 128), 128)

    hid_out, hid_in, fwd_out, fwd_in = [], [], [], []
    for i in range(8):
        hid_out.append(
            rc(
                hid_ref.at[hid_rows(1 - h, i, 1 - g), :],
                oth.at[loc_rows(i, 1 - g), :],
                hid_ss.at[i],
                hid_rs.at[i],
                cross_dev,
            )
        )
        mine = oth.at[loc_rows(i, g), :]
        theirs = oth.at[loc_rows(i, 1 - g), :]
        hid_in.append(rc(mine, mine, hid_ss.at[i], hid_rs.at[i], cross_dev))
        fwd_out.append(rc(mine, mine, fwd_ss.at[i], fwd_rs.at[i], grp_dev))
        fwd_in.append(rc(theirs, theirs, fwd_ss.at[i], fwd_rs.at[i], grp_dev))
    for i in range(8):
        hid_out[i].start()

    @pl.loop(0, 8)
    def _(i):
        rows = pl.ds(pl.multiple_of(i * 32, 32), 32)
        wide = stu_ref[rows, :].astype(F32)
        scale = lax.rsqrt(jnp.sum(wide * wide, axis=1, keepdims=True) / DS + norm_eps)
        done = (wide * scale * sgain_ref[...]).astype(BF16)
        for b in range(8):
            nrm[b, rows, :] = done[:, b * 512 : (b + 1) * 512]

    def nrm_out(xx, cc):
        to = xx * 2 + cc
        return rc(nrm.at[to], nall.at[dp], nrm_ss.at[to], nrm_rs.at[dp], at(xx=xx, cc=cc))

    def nrm_in(xx, cc):
        fr = xx * 2 + cc
        return rc(nall.at[fr], nall.at[fr], nrm_ss.at[fr], nrm_rs.at[fr], at(xx=xx, cc=cc))

    nrm_own = pltpu.make_async_copy(nrm.at[dp], nall.at[dp], loc_sem.at[2])
    nrm_own.start()
    nrm_out(x, 1 - c).start()
    for e in (1, 3):
        for cc in range(2):
            nrm_out(xp(e), cc).start()

    w_cp.wait()
    w_far_in.wait_recv()

    def wpiece(d):
        return wgt.at[dp, :, pl.ds(pl.multiple_of(zp(d) * 32, 32), 32), :]

    def wz_out(way, s):
        sign = 1 if way == 0 else -1
        piece = wpiece(-sign * s)
        return rc(piece, piece, wz_ss.at[way, s], wz_rs.at[way, s], at(zz=zp(sign)))

    def wz_in(way, s):
        sign = 1 if way == 0 else -1
        piece = wpiece(-sign * (s + 1))
        return rc(piece, piece, wz_ss.at[way, s], wz_rs.at[way, s], at(zz=zp(sign)))

    def wz_step(s):
        if s > 0:
            wz_in(0, s - 1).wait_recv()
            wz_in(1, s - 1).wait_recv()
        wz_out(0, s).start()
        if s < 3:
            wz_out(1, s).start()

    def wblock(xx, cc=None):
        return wgt.at[xx * 2 + (c if cc is None else cc)]

    def wx_out(way):
        return rc(wblock(x), wblock(x), wx_ss.at[way], wx_rs.at[way], at(xx=xp(1 if way == 0 else -1)))

    def wx_in(way):
        b = wblock(xp(-1 if way == 0 else 1))
        return rc(b, b, wx_ss.at[way], wx_rs.at[way], at(xx=xp(1 if way == 0 else -1)))

    def wx_fw(way):
        b = wblock(xp(-1 if way == 0 else 1)).at[way]
        return rc(b, b, wx_ss.at[2 + way], wx_rs.at[2 + way], at(xx=xp(1 if way == 0 else -1)))

    def wx_fin(way):
        b = wblock(xp(2)).at[way]
        return rc(b, b, wx_ss.at[2 + way], wx_rs.at[2 + way], at(xx=xp(1 if way == 0 else -1)))

    def wc_out(e):
        b = wblock(xp(e))
        return rc(b, b, wc_ss.at[e], wc_rs.at[e], core_dev)

    def wc_in(e):
        b = wblock(xp(e), 1 - c)
        return rc(b, b, wc_ss.at[e], wc_rs.at[e], core_dev)

    wz_step(0)

    seg = seg_ref[pl.ds(mp // 4, 1), :]
    lens = jnp.zeros((1, 1024), F32)
    for s in range(NSEG):
        hit = (seg == s).astype(F32)
        lens = lens + hit * jnp.sum(hit, axis=1, keepdims=True)
    len_row[0:1, :] = lens

    eye = lax.broadcasted_iota(jnp.int32, (128, 128), 0) == lax.broadcasted_iota(
        jnp.int32, (128, 128), 1
    )

    def to_row(col):
        return jnp.sum(jnp.where(eye, col, 0.0), axis=0, keepdims=True)

    def to_col(row):
        return jnp.sum(jnp.where(eye, row, 0.0), axis=1, keepdims=True)

    val_cp.wait_recv()
    val_fw.start()
    own_cp.wait()

    def ring_cp(way, s):
        if s == 0:
            cols = pl.ds(way * 256, 256)
            src, dst = ring_s.at[way, s, :, cols], ring_r.at[way, s, :, cols]
        else:
            src, dst = ring_s.at[way, s], ring_r.at[way, s]
        dev = at(zz=zp(1 if way == 0 else -1))
        return rc(src, dst, ring_ss.at[way, s], ring_rs.at[way, s], dev)

    def sq_out(d):
        return rc(sq_s.at[zp(d)], sq_r.at[z], sq_ss.at[zp(d)], sq_rs.at[z], at(zz=zp(d)))

    def sq_in(d):
        return rc(sq_r.at[zp(d)], sq_r.at[zp(d)], sq_ss.at[zp(d)], sq_rs.at[zp(d)], at(zz=zp(d)))

    def chunk(i):
        d = ORDER[i]
        k = zp(d)
        fwd_in[i].wait_recv()
        if d not in (4, 0):
            ring_cp(0 if d > 0 else 1, 3 - abs(d)).wait_recv()
        if d == 0:
            ring_cp(0, 3).wait_recv()
            ring_cp(1, 3).wait_recv()

        @pl.loop(0, 2)
        def _(j):
            rows = pl.ds(pl.multiple_of(k * 256 + j * 128, 128), 128)
            brows = pl.ds(pl.multiple_of(j * 128, 128), 128)
            h1 = own[rows, :].astype(F32)
            h2 = oth[rows, :].astype(F32)
            acc = jnp.dot(
                (h1 * gain_ref[...]).astype(BF16), val_ref[...], preferred_element_type=F32
            )
            acc += jnp.dot((h2 * gaino[...]).astype(BF16), valo[...], preferred_element_type=F32)
            sq = jnp.sum(h1 * h1 + h2 * h2, axis=1, keepdims=True)
            sq_s[k, pl.ds(j, 1), :] = to_row(sq)
            if d == 4:
                ring_s[0, 0, brows, 0:256] = acc[:, 0:256].astype(BF16)
                ring_s[1, 0, brows, 256:512] = acc[:, 256:512].astype(BF16)
            elif d == 0:
                total[brows, :] = (
                    acc + ring_r[0, 3, brows, :].astype(F32) + ring_r[1, 3, brows, :].astype(F32)
                )
            else:
                way, s = (0 if d > 0 else 1), 4 - abs(d)
                if s == 1:
                    cols = slice(way * 256, way * 256 + 256)
                    rest = slice((1 - way) * 256, (1 - way) * 256 + 256)
                    ring_s[way, s, brows, cols] = (
                        acc[:, cols] + ring_r[way, 0, brows, cols].astype(F32)
                    ).astype(BF16)
                    ring_s[way, s, brows, rest] = acc[:, rest].astype(BF16)
                else:
                    ring_s[way, s, brows, :] = (
                        acc + ring_r[way, s - 1, brows, :].astype(F32)
                    ).astype(BF16)

        if d == 4:
            ring_cp(0, 0).start()
            ring_cp(1, 0).start()
        elif d != 0:
            ring_cp(0 if d > 0 else 1, 4 - abs(d)).start()
        if d != 0:
            sq_out(d).start()

    for i in range(9):
        if i < 8:
            hid_in[i].wait_recv()
            fwd_out[i].start()
        if i == 1:
            wz_step(1)
            wz_step(2)
            val_in.wait_recv()
            gain_cp.wait_recv()
        if i == 2:
            wz_step(3)
        if i == 3:
            wz_in(0, 3).wait_recv()
            wx_out(0).start()
            wx_out(1).start()
            wc_out(0).start()
        if i == 7:
            for way in range(2):
                wx_in(way).wait_recv()
                wx_fw(way).start()
            wc_out(1).start()
            wc_out(3).start()
            for cc in range(2):
                nrm_out(xp(2), cc).start()
        if i == 8:
            wx_fin(0).wait_recv()
            wx_fin(1).wait_recv()
            wc_out(2).start()
            for e in range(4):
                wc_in(e).wait_recv()
            states[...] = jnp.zeros_like(states)

            @pl.loop(0, 8)
            def _(b):
                for hh in range(2):
                    states[...] += jnp.dot(
                        nrm[b, :, hh * 256 : hh * 256 + 256],
                        wgt[b, hh],
                        preferred_element_type=F32,
                    )

        if i >= 1:
            chunk(i - 1)

    for d in range(1, 8):
        sq_in(d).wait_recv()
    sq_r[z] = sq_s[z]
    rows_sq = jnp.zeros((8, 128), F32)
    for s in range(8):
        rows_sq = rows_sq + sq_r[s]
    for j in range(2):
        rows = slice(j * 128, (j + 1) * 128)
        scale = lax.rsqrt(to_col(rows_sq[j : j + 1, :]) / DT + norm_eps)
        target = total[rows, :] * scale
        total[rows, :] = target
        pow_s[j : j + 1, :] = to_row(jnp.sum(target * target, axis=1, keepdims=True))
    pow_cp = rc(pow_s, pow_r, misc_ss.at[4], misc_rs.at[4], grp_dev)
    pow_cp.start()
    pow_cp.wait_recv()
    for j in range(2):
        rows = slice(j * 128, (j + 1) * 128)
        power = (pow_s[j : j + 1, :] + pow_r[j : j + 1, :]) / KV + power_eps
        length = len_row[0:1, pl.ds(pl.multiple_of((mp % 4) * 256 + j * 128, 128), 128)]
        div = to_col(length * power)
        wall[dp, rows, :] = ((states[rows, :] - total[rows, :]) / div).astype(BF16)

    def wal_out(e):
        b = wall.at[dp]
        return rc(b, b, wal_ss.at[e - 1], wal_rs.at[e - 1], at(xx=xp(e)))

    def wal_in(e):
        b = wall.at[xp(-e) * 2 + c]
        return rc(b, b, wal_ss.at[e - 1], wal_rs.at[e - 1], at(xx=xp(e)))

    def wac_out(e):
        b = wall.at[xp(-e) * 2 + c]
        return rc(b, b, wac_ss.at[e], wac_rs.at[e], core_dev)

    def wac_in(e):
        b = wall.at[xp(-e) * 2 + 1 - c]
        return rc(b, b, wac_ss.at[e], wac_rs.at[e], core_dev)

    for e in (1, 3, 2):
        wal_out(e).start()
    wac_out(0).start()
    nrm_own.wait()

    def accumulate(slot, first=False):
        part = lax.dot_general(
            nall[slot], wall[slot], (((0,), (0,)), ((), ())), preferred_element_type=F32
        )
        if first:
            grad[...] = part
        else:
            grad[...] += part

    accumulate(dp, True)
    nrm_in(x, 1 - c).wait_recv()
    wac_in(0).wait_recv()
    accumulate(x * 2 + 1 - c)
    for e in (1, 3, 2):
        for cc in range(2):
            nrm_in(xp(-e), cc).wait_recv()
        wal_in(e).wait_recv()
        wac_out(e).start()
        accumulate(xp(-e) * 2 + c)
        wac_in(e).wait_recv()
        accumulate(xp(-e) * 2 + 1 - c)

    for b in range(16):
        grad_s[b] = grad[b * 32 : (b + 1) * 32, :].astype(BF16)

    def grad_out(t):
        to = lax.rem(mp + t, 16)
        return rc(grad_s.at[to], grad_r.at[mp], grad_ss.at[to], grad_rs.at[mp], (g, dp, to))

    def grad_in(t):
        fr = lax.rem(mp + t, 16)
        return rc(grad_r.at[fr], grad_r.at[fr], grad_ss.at[fr], grad_rs.at[fr], (g, dp, fr))

    for t in range(1, 16):
        grad_out(t).start()
    acc = grad[pl.ds(pl.multiple_of(mp * 32, 32), 32), :]
    for t in range(1, 16):
        grad_in(t).wait_recv()
    for t in range(1, 16):
        acc = acc + grad_r[lax.rem(mp + t, 16)].astype(F32)
    out_ref[...] = acc

    val_cp.wait_send()
    val_fw.wait_send()
    gain_cp.wait_send()
    w_far.wait_send()
    pow_cp.wait_send()
    for i in range(8):
        hid_out[i].wait_send()
        fwd_out[i].wait_send()
    for s in range(4):
        wz_out(0, s).wait_send()
        if s < 3:
            wz_out(1, s).wait_send()
        ring_cp(0, s).wait_send()
        ring_cp(1, s).wait_send()
    for way in range(2):
        wx_out(way).wait_send()
        wx_fw(way).wait_send()
    for e in range(4):
        wc_out(e).wait_send()
        wac_out(e).wait_send()
    nrm_out(x, 1 - c).wait_send()
    for e in range(1, 4):
        wal_out(e).wait_send()
        for cc in range(2):
            nrm_out(xp(e), cc).wait_send()
    for d in range(1, 8):
        sq_out(d).wait_send()
    for t in range(1, 16):
        grad_out(t).wait_send()


def per_device(
    teacher_hidden,
    teacher_gain,
    teacher_value,
    student_hidden,
    student_gain,
    student_value,
    segment_ids,
):
    vmem = pl.BlockSpec(memory_space=pltpu.VMEM)
    dma = pltpu.SemaphoreType.DMA
    return pl.pallas_call(
        kernel,
        out_shape=jax.ShapeDtypeStruct((32, 512), F32),
        in_specs=[pl.BlockSpec(memory_space=pl.ANY)] + [vmem] * 6,
        out_specs=vmem,
        scratch_shapes=[
            pltpu.VMEM((2048, 512), BF16),
            pltpu.VMEM((2048, 512), BF16),
            pltpu.VMEM((512, 512), BF16),
            pltpu.VMEM((1, 512), F32),
            pltpu.VMEM((8, 256, 512), BF16),
            pltpu.VMEM((8, 256, 512), BF16),
            pltpu.VMEM((8, 2, 256, 512), BF16),
            pltpu.VMEM((2, 4, 256, 512), BF16),
            pltpu.VMEM((2, 4, 256, 512), BF16),
            pltpu.VMEM((8, 8, 128), F32),
            pltpu.VMEM((8, 8, 128), F32),
            pltpu.VMEM((256, 512), F32),
            pltpu.VMEM((256, 512), F32),
            pltpu.VMEM((8, 128), F32),
            pltpu.VMEM((8, 128), F32),
            pltpu.VMEM((8, 1024), F32),
            pltpu.VMEM((8, 256, 512), BF16),
            pltpu.VMEM((512, 512), F32),
            pltpu.VMEM((16, 32, 512), BF16),
            pltpu.VMEM((16, 32, 512), BF16),
            dma((3,)),
            dma((8,)),
            dma((8,)),
            dma((8,)),
            dma((8,)),
            dma((5,)),
            dma((5,)),
            dma((2, 4)),
            dma((2, 4)),
            dma((4,)),
            dma((4,)),
            dma((4,)),
            dma((4,)),
            dma((8,)),
            dma((8,)),
            dma((2, 4)),
            dma((2, 4)),
            dma((8,)),
            dma((8,)),
            dma((3,)),
            dma((3,)),
            dma((4,)),
            dma((4,)),
            dma((16,)),
            dma((16,)),
        ],
        compiler_params=pltpu.CompilerParams(
            collective_id=0, has_side_effects=True, vmem_limit_bytes=56 * 1024 * 1024
        ),
    )(
        teacher_hidden,
        teacher_gain.astype(F32).reshape(1, -1),
        teacher_value,
        student_hidden,
        student_gain.astype(F32).reshape(1, -1),
        student_value,
        segment_ids,
    )


def solution(mesh):
    return jax.shard_map(
        per_device,
        mesh=mesh,
        in_specs=(
            P("dp", "mp"),
            P("mp"),
            P("mp", "grp"),
            P(("dp", "mp"), None),
            P(),
            P(("dp", "mp"), "grp"),
            P("dp", None),
        ),
        out_specs=P(("dp", "mp"), "grp"),
        check_vma=False,
    )
```

time: 945 us -> 110 us (0.12)
  waiting for transfers between devices: 822 us -> 0 us
  Pallas kernels: 0 us -> 105 us
  blocking collectives: 84.7 us -> 0 us
  matrix products: 15.8 us -> 0 us
  between operations: 15.6 us -> 0.01 us
    reduce_scatter x2 -> x0, waiting for transfers between devices: 821 us -> none  [the longest x1 679 us: per_device(): lax.psum_scatter(lax.dot_general(row_block, weighted, (((0,), (0,)), ((),...]
    pallas_call x0 -> x1, Pallas kernels: none -> 105 us  [per_device(): pl.pallas_call(kernel, out_shape=jax.ShapeDtypeStruct((32, 512), F32), in...]
    unnamed x1 -> x0, blocking collectives: 79.8 us -> none
    dot_general x2 -> x0, matrix products: 15.8 us -> none  [the longest x1 8.08 us: per_device(): lax.dot_general(row_block, weighted, (((0,), (0,)), ((), ())), preferred_...]
  transfers between devices with their start and end apart: 3 -> 0, of which waited for: 2 -> 0; matrix products, arithmetic and copies ran while one was open for 1% -> 0% of each run, Pallas kernels for 0% -> 0%
where the time goes in v1:
time: 110 us; the launch traced here: 109 us
  Pallas kernels  105 us (95%)
  other arithmetic  2.55 us (2%)
  local copies, waits for them, and re-layouts  1.47 us (1%)
    pallas_call x1, Pallas kernels, per_device(): pl.pallas_call(kernel, out_shape=jax.ShapeDtypeStruct((32, 512), F32), in...  105 us

profile of v1, /device:TPU:8, one launch (start us, length us, event | category | flops | bytes accessed | tf_op | source)
XLA Modules:
  0.0 108.7 jit_solution(14757174035979450278)
XLA Ops:
  0.0 1.2 %reshape.14 = f32[512]{0:T(512)} convert(bf16[512]{0:T(512)(128)(2,1)} %param.8) | non-fusion elementwise | flops 512 | bytes 3072 | tf_op jit(solution)/shard_map/reshape | solution.py:559
  1.2 1.3 %reshape.16 = f32[4096]{0:T(1024)} convert(bf16[4096]{0:T(1024)(128)(2,1)} %param.11) | non-fusion elementwise | flops 4096 | bytes 24576 | tf_op jit(solution)/shard_map/reshape | solution.py:562
  2.5 104.7 %shard_map.73 = f32[32,512]{1,0:T(8,128)} custom-call(bf16[4096,512]{1,0:T(8,128)(2,1)} %hid_ref.1, f32[1,512]{1,0:T(1,128)} %bitcast.3, bf16[512,512]{1,0:T(8,128)(2,1)} %val_ref.1, bf16[256,4096]{1,0:T(8,128)(2,1)} %stu_ref.1, f32[1,4096]{1,0:T(1,128)} %bitcast.2, bf16[32,512]{1,0:T(8,128)(2,1)} %wsh_ref.1, s32[4,1024]{1,0:T(4,128)} %seg_ref.1), custom_call_target="tpu_custom_call" | custom-call | tf_op jit(solution)/shard_map/pallas_call | solution.py:502
  107.2 1.5 %copy.9 = f32[32,512]{1,0:T(8,128)} copy(f32[32,512]{1,0:T(8,128)} %shard_map.73) | data formatting | bytes 131072

commit v2 on v1

v2 whole, which is shorter than its diff:
```python
import jax
import jax.numpy as jnp
from jax import lax
from jax.experimental import pallas as pl
from jax.experimental.pallas import tpu as pltpu
from jax.sharding import PartitionSpec as P

DT = 8192
DS = 4096
KV = 1024
NSEG = 8
MESH = pl.DeviceIdType.MESH
F32 = jnp.float32
BF16 = jnp.bfloat16

norm_eps = 1e-05
power_eps = 1e-06

ORDER = (4, 3, -3, 2, -2, 1, -1, 0)
NEAR = (4, 3, -3, 2, -2, 1, -1)


def kernel(
    hid_ref,
    gain_ref,
    val_ref,
    stu_ref,
    sgain_ref,
    wsh_ref,
    seg_ref,
    out_ref,
    own,
    oth,
    valo,
    valt,
    gaino,
    nrm,
    nall,
    wgt,
    ring_s,
    ring_r,
    sq_s,
    sq_r,
    states,
    total,
    pow_s,
    pow_r,
    len_row,
    wall,
    grad,
    grad_s,
    grad_r,
    loc_sem,
    hid_ss,
    hid_rs,
    fwd_ss,
    fwd_rs,
    misc_ss,
    misc_rs,
    val_ss,
    val_rs,
    wz_ss,
    wz_rs,
    wx_ss,
    wx_rs,
    wc_ss,
    wc_rs,
    nrm_ss,
    nrm_rs,
    ring_ss,
    ring_rs,
    sq_ss,
    sq_rs,
    wal_ss,
    wal_rs,
    wac_ss,
    wac_rs,
    grad_ss,
    grad_rs,
):
    g = lax.axis_index("grp")
    dp = lax.axis_index("dp")
    mp = lax.axis_index("mp")
    x, c = dp // 2, dp % 2
    h, z = mp // 8, mp % 8

    def at(grp=None, xx=None, cc=None, hh=None, zz=None):
        return (
            g if grp is None else grp,
            (x if xx is None else xx) * 2 + (c if cc is None else cc),
            (h if hh is None else hh) * 8 + (z if zz is None else zz),
        )

    def rc(src, dst, ss, rs, dev):
        return pltpu.make_async_remote_copy(
            src_ref=src, dst_ref=dst, send_sem=ss, recv_sem=rs, device_id=dev, device_id_type=MESH
        )

    zp = lambda d: lax.rem(z + d + 8, 8)
    xp = lambda e: lax.rem(x + e + 4, 4)
    grp_dev = at(grp=1 - g)
    cross_dev = at(grp=1 - g, hh=1 - h)
    far_dev = at(hh=1 - h)
    core_dev = at(cc=1 - c)

    own_cp = pltpu.make_async_copy(
        hid_ref.at[pl.ds(pl.multiple_of(h * 2048, 2048), 2048), :], own, loc_sem.at[0]
    )
    own_cp.start()
    w_cp = pltpu.make_async_copy(
        wsh_ref, wgt.at[dp, h, pl.ds(pl.multiple_of(z * 32, 32), 32), :], loc_sem.at[1]
    )
    w_cp.start()

    barrier = pltpu.get_barrier_semaphore()
    count = 0
    for d in range(1, 8):
        pl.semaphore_signal(barrier, inc=1, device_id=at(zz=zp(d)), device_id_type=MESH)
        count += 1
    for d in range(8):
        pl.semaphore_signal(barrier, inc=1, device_id=at(hh=1 - h, zz=zp(d)), device_id_type=MESH)
        count += 1
    for e in range(1, 4):
        for cc in range(2):
            pl.semaphore_signal(
                barrier, inc=1, device_id=at(xx=xp(e), cc=cc), device_id_type=MESH
            )
            count += 1
    for dev in (grp_dev, cross_dev, core_dev):
        pl.semaphore_signal(barrier, inc=1, device_id=dev, device_id_type=MESH)
        count += 1

    sgain = sgain_ref[...].astype(F32).reshape(1, DS)

    @pl.loop(0, 8)
    def _(i):
        rows = pl.ds(pl.multiple_of(i * 32, 32), 32)
        wide = stu_ref[rows, :].astype(F32)
        scale = lax.rsqrt(jnp.sum(wide * wide, axis=1, keepdims=True) / DS + norm_eps)
        done = (wide * scale * sgain).astype(BF16)
        for b in range(8):
            nrm[b, rows, :] = done[:, b * 512 : (b + 1) * 512]

    nrm_own = pltpu.make_async_copy(nrm.at[dp], nall.at[dp], loc_sem.at[2])
    nrm_own.start()

    seg = seg_ref[pl.ds(mp // 4, 1), :]
    lens = jnp.zeros((1, 1024), F32)
    for s in range(NSEG):
        hit = (seg == s).astype(F32)
        lens = lens + hit * jnp.sum(hit, axis=1, keepdims=True)
    len_row[0:1, :] = lens

    eye = lax.broadcasted_iota(jnp.int32, (128, 128), 0) == lax.broadcasted_iota(
        jnp.int32, (128, 128), 1
    )

    def to_row(col):
        return jnp.sum(jnp.where(eye, col, 0.0), axis=0, keepdims=True)

    def to_col(row):
        return jnp.sum(jnp.where(eye, row, 0.0), axis=1, keepdims=True)

    pl.semaphore_wait(barrier, count)

    def wz_piece(hh, d):
        return wgt.at[dp, hh, pl.ds(pl.multiple_of(zp(d) * 32, 32), 32), :]

    def wz_out(b, d):
        src = wsh_ref if b == 0 else wz_piece(1 - h, 0)
        dst = wz_piece(h if b == 0 else 1 - h, 0)
        return rc(src, dst, wz_ss.at[b, zp(d)], wz_rs.at[b, z], at(zz=zp(d)))

    def wz_in(b, d):
        piece = wz_piece(h if b == 0 else 1 - h, d)
        return rc(piece, piece, wz_ss.at[b, zp(d)], wz_rs.at[b, zp(d)], at(zz=zp(d)))

    wrow = lambda hh: wz_piece(hh, 0)
    w_far = rc(wsh_ref, wrow(h), misc_ss.at[3], misc_rs.at[3], far_dev)
    w_far_in = rc(wsh_ref, wrow(1 - h), misc_ss.at[3], misc_rs.at[3], far_dev)
    w_far.start()
    hop1_dev = at(grp=1 - g, hh=(1 - h) * (1 - c) + h * c)
    hop2_dev = at(grp=1 - g, hh=h * (1 - c) + (1 - h) * c)

    def vrows(cc, p):
        return pl.ds(pl.multiple_of(cc * 256 + p * 128, 128), 128)

    val_cp, val_h2, val_fw, val_in = [], [], [], []
    for p in range(2):
        tmp = valt.at[pl.ds(p * 128, 128), :]
        mine, theirs = valo.at[vrows(c, p), :], valo.at[vrows(1 - c, p), :]
        val_cp.append(rc(val_ref.at[vrows(c, p), :], tmp, val_ss.at[0, p], val_rs.at[0, p], hop1_dev))
        val_h2.append(rc(tmp, mine, val_ss.at[1, p], val_rs.at[1, p], hop2_dev))
        val_fw.append(rc(mine, mine, val_ss.at[2, p], val_rs.at[2, p], core_dev))
        val_in.append(rc(theirs, theirs, val_ss.at[2, p], val_rs.at[2, p], core_dev))
        val_cp[p].start()
    gain_cp = rc(gain_ref, gaino, misc_ss.at[2], misc_rs.at[2], cross_dev)
    gain_cp.start()

    def hid_rows(hh, i, j):
        return pl.ds(pl.multiple_of(hh * 2048 + zp(ORDER[i]) * 256 + j * 128, 128), 128)

    def loc_rows(i, j):
        return pl.ds(pl.multiple_of(zp(ORDER[i]) * 256 + j * 128, 128), 128)

    hid_out, hid_in, fwd_out, fwd_in = [], [], [], []
    for i in range(8):
        hid_out.append(
            rc(
                hid_ref.at[hid_rows(1 - h, i, 1 - g), :],
                oth.at[loc_rows(i, 1 - g), :],
                hid_ss.at[i],
                hid_rs.at[i],
                cross_dev,
            )
        )
        mine = oth.at[loc_rows(i, g), :]
        theirs = oth.at[loc_rows(i, 1 - g), :]
        hid_in.append(rc(mine, mine, hid_ss.at[i], hid_rs.at[i], cross_dev))
        fwd_out.append(rc(mine, mine, fwd_ss.at[i], fwd_rs.at[i], grp_dev))
        fwd_in.append(rc(theirs, theirs, fwd_ss.at[i], fwd_rs.at[i], grp_dev))
    for d in NEAR:
        wz_out(0, d).start()
    hid_out[0].start()

    def nrm_out(xx, cc):
        to = xx * 2 + cc
        return rc(nrm.at[to], nall.at[dp], nrm_ss.at[to], nrm_rs.at[dp], at(xx=xx, cc=cc))

    def nrm_in(xx, cc):
        fr = xx * 2 + cc
        return rc(nall.at[fr], nall.at[fr], nrm_ss.at[fr], nrm_rs.at[fr], at(xx=xx, cc=cc))

    nrm_out(x, 1 - c).start()
    for e in (1, 3):
        for cc in range(2):
            nrm_out(xp(e), cc).start()
    nrm_out(xp(2), c).start()

    def wblock(xx, cc=None):
        return wgt.at[xx * 2 + (c if cc is None else cc)]

    def wx_dev(way):
        return at(xx=xp(1 if way == 0 else -1))

    def wx_out(way):
        return rc(wblock(x), wblock(x), wx_ss.at[way], wx_rs.at[way], wx_dev(way))

    def wx_in(way):
        b = wblock(xp(-1 if way == 0 else 1))
        return rc(b, b, wx_ss.at[way], wx_rs.at[way], wx_dev(way))

    def wx_fw(way):
        b = wblock(xp(-1 if way == 0 else 1)).at[way]
        return rc(b, b, wx_ss.at[2 + way], wx_rs.at[2 + way], wx_dev(way))

    def wx_fin(way):
        b = wblock(xp(2)).at[way]
        return rc(b, b, wx_ss.at[2 + way], wx_rs.at[2 + way], wx_dev(way))

    def wc_out(e):
        b = wblock(xp(e))
        return rc(b, b, wc_ss.at[e], wc_rs.at[e], core_dev)

    def wc_in(e):
        b = wblock(xp(e), 1 - c)
        return rc(b, b, wc_ss.at[e], wc_rs.at[e], core_dev)

    def ring_cp(way, s, u):
        rows = pl.ds(pl.multiple_of((g if u == 0 else 1 - g) * 128, 128), 128)
        cols = pl.ds(way * 256, 256) if s == 0 else pl.ds(0, 512)
        dev = at(zz=zp(1 if way == 0 else -1))
        return rc(
            ring_s.at[way, s, rows, cols],
            ring_r.at[way, s, rows, cols],
            ring_ss.at[way, s, u],
            ring_rs.at[way, s, u],
            dev,
        )

    def sq_out(d):
        return rc(sq_s.at[zp(d)], sq_r.at[z], sq_ss.at[zp(d)], sq_rs.at[z], at(zz=zp(d)))

    def sq_in(d):
        return rc(sq_r.at[zp(d)], sq_r.at[zp(d)], sq_ss.at[zp(d)], sq_rs.at[zp(d)], at(zz=zp(d)))

    def sub(i, u):
        d = ORDER[i]
        k = zp(d)
        j = g if u == 0 else 1 - g
        if u == 1:
            fwd_in[i].wait_recv()
        if d == 0:
            ring_cp(0, 3, u).wait_recv()
            ring_cp(1, 3, u).wait_recv()
        elif d != 4:
            ring_cp(0 if d > 0 else 1, 3 - abs(d), u).wait_recv()
        rows = pl.ds(pl.multiple_of(k * 256 + j * 128, 128), 128)
        brows = pl.ds(pl.multiple_of(j * 128, 128), 128)
        h1 = own[rows, :].astype(F32)
        h2 = oth[rows, :].astype(F32)
        tgain = gain_ref[...].astype(F32).reshape(1, 512)
        tgaino = gaino[...].astype(F32).reshape(1, 512)
        acc = jnp.dot((h1 * tgain).astype(BF16), val_ref[...], preferred_element_type=F32)
        acc += jnp.dot((h2 * tgaino).astype(BF16), valo[...], preferred_element_type=F32)
        if d == 4:
            ring_s[0, 0, brows, 0:256] = acc[:, 0:256].astype(BF16)
            ring_s[1, 0, brows, 256:512] = acc[:, 256:512].astype(BF16)
            ring_cp(0, 0, u).start()
            ring_cp(1, 0, u).start()
        elif d == 0:
            total[brows, :] = (
                acc + ring_r[0, 3, brows, :].astype(F32) + ring_r[1, 3, brows, :].astype(F32)
            )
        else:
            way, s = (0 if d > 0 else 1), 4 - abs(d)
            if s == 1:
                cols = slice(way * 256, way * 256 + 256)
                rest = slice((1 - way) * 256, (1 - way) * 256 + 256)
                ring_s[way, s, brows, cols] = (
                    acc[:, cols] + ring_r[way, 0, brows, cols].astype(F32)
                ).astype(BF16)
                ring_s[way, s, brows, rest] = acc[:, rest].astype(BF16)
            else:
                ring_s[way, s, brows, :] = (
                    acc + ring_r[way, s - 1, brows, :].astype(F32)
                ).astype(BF16)
            ring_cp(way, s, u).start()
        sq = jnp.sum(h1 * h1 + h2 * h2, axis=1, keepdims=True)
        sq_s[k, pl.ds(j, 1), :] = to_row(sq)
        if u == 1 and d != 0:
            sq_out(d).start()

    def take(i):
        hid_in[i].wait_recv()
        fwd_out[i].start()
        if i + 3 < 8:
            hid_out[i + 3].start()

    def add_states(blocks):
        part = None
        for b in blocks:
            for hh in range(2):
                t = jnp.dot(
                    nrm[b, :, hh * 256 : hh * 256 + 256], wgt[b, hh], preferred_element_type=F32
                )
                part = t if part is None else part + t
        states[...] += part

    states[...] = jnp.zeros_like(states)
    w_far_in.wait_recv()
    for d in NEAR:
        wz_out(1, d).start()
    for p in range(2):
        val_cp[p].wait_recv()
        val_h2[p].start()
    hid_out[1].start()
    hid_out[2].start()
    take(0)
    for p in range(2):
        val_h2[p].wait_recv()
        val_fw[p].start()
    own_cp.wait()
    w_cp.wait()
    gain_cp.wait_recv()
    for p in range(2):
        val_in[p].wait_recv()
    sub(0, 0)
    for b in range(2):
        for d in NEAR:
            wz_in(b, d).wait_recv()
    wx_out(0).start()
    wx_out(1).start()
    wc_out(0).start()
    take(1)
    take(2)
    sub(0, 1)
    sub(1, 0)
    sub(2, 0)
    take(3)
    sub(1, 1)
    sub(2, 1)
    take(4)
    sub(3, 0)
    sub(4, 0)
    for way in range(2):
        wx_in(way).wait_recv()
        wx_fw(way).start()
    wc_out(1).start()
    wc_out(3).start()
    take(5)
    sub(3, 1)
    sub(4, 1)
    take(6)
    add_states((xp(1) * 2 + c, xp(-1) * 2 + c))
    wc_in(0).wait_recv()
    add_states((dp, x * 2 + 1 - c))
    sub(5, 0)
    sub(6, 0)
    take(7)
    sub(5, 1)
    sub(6, 1)
    wx_fin(0).wait_recv()
    wx_fin(1).wait_recv()
    wc_out(2).start()
    nrm_out(xp(2), 1 - c).start()
    wc_in(1).wait_recv()
    wc_in(3).wait_recv()
    add_states((xp(1) * 2 + 1 - c, xp(-1) * 2 + 1 - c))
    sub(7, 0)
    sub(7, 1)
    wc_in(2).wait_recv()
    add_states((xp(2) * 2, xp(2) * 2 + 1))

    for d in range(1, 8):
        sq_in(d).wait_recv()
    sq_r[z] = sq_s[z]
    rows_sq = jnp.zeros((8, 128), F32)
    for s in range(8):
        rows_sq = rows_sq + sq_r[s]
    for j in range(2):
        rows = slice(j * 128, (j + 1) * 128)
        scale = lax.rsqrt(to_col(rows_sq[j : j + 1, :]) / DT + norm_eps)
        target = total[rows, :] * scale
        total[rows, :] = states[rows, :] - target
        pow_s[j : j + 1, :] = to_row(jnp.sum(target * target, axis=1, keepdims=True))
    pow_cp = rc(pow_s, pow_r, misc_ss.at[4], misc_rs.at[4], grp_dev)
    pow_cp.start()

    def wal_out(q, e):
        b = wall.at[q, dp]
        return rc(b, b, wal_ss.at[q, e - 1], wal_rs.at[q, e - 1], at(xx=xp(e)))

    def wal_in(q, e):
        b = wall.at[q, xp(-e) * 2 + c]
        return rc(b, b, wal_ss.at[q, e - 1], wal_rs.at[q, e - 1], at(xx=xp(e)))

    def wac_out(q, e):
        b = wall.at[q, xp(-e) * 2 + c]
        return rc(b, b, wac_ss.at[q, e], wac_rs.at[q, e], core_dev)

    def wac_in(q, e):
        b = wall.at[q, xp(-e) * 2 + 1 - c]
        return rc(b, b, wac_ss.at[q, e], wac_rs.at[q, e], core_dev)

    def grad_out(q, t):
        to = lax.rem(mp + t, 16)
        return rc(
            grad_s.at[q, to], grad_r.at[q, mp], grad_ss.at[q, to], grad_rs.at[q, mp], (g, dp, to)
        )

    def grad_in(q, t):
        fr = lax.rem(mp + t, 16)
        return rc(
            grad_r.at[q, fr], grad_r.at[q, fr], grad_ss.at[q, fr], grad_rs.at[q, fr], (g, dp, fr)
        )

    pow_cp.wait_recv()
    divs = []
    for j in range(2):
        power = (pow_s[j : j + 1, :] + pow_r[j : j + 1, :]) / KV + power_eps
        length = len_row[0:1, pl.ds(pl.multiple_of((mp % 4) * 256 + j * 128, 128), 128)]
        divs.append(to_col(length * power))
    for q in range(2):
        for j in range(2):
            rows = slice(j * 128, (j + 1) * 128)
            wall[q, dp, rows, :] = (total[rows, q * 256 : q * 256 + 256] / divs[j]).astype(BF16)
        for e in (1, 3, 2):
            wal_out(q, e).start()
        wac_out(q, 0).start()

    nrm_own.wait()
    nrm_in(x, 1 - c).wait_recv()
    for e in (1, 3, 2):
        for cc in range(2):
            nrm_in(xp(-e), cc).wait_recv()

    def accumulate(q, slot):
        grad[...] += lax.dot_general(
            nall[slot], wall[q, slot], (((0,), (0,)), ((), ())), preferred_element_type=F32
        )

    for q in range(2):
        grad[...] = jnp.zeros_like(grad)
        accumulate(q, dp)
        wac_in(q, 0).wait_recv()
        accumulate(q, x * 2 + 1 - c)
        wal_in(q, 1).wait_recv()
        wac_out(q, 1).start()
        accumulate(q, xp(-1) * 2 + c)
        wal_in(q, 3).wait_recv()
        wac_out(q, 3).start()
        accumulate(q, xp(-3) * 2 + c)
        wac_in(q, 1).wait_recv()
        accumulate(q, xp(-1) * 2 + 1 - c)
        wal_in(q, 2).wait_recv()
        wac_out(q, 2).start()
        accumulate(q, xp(-2) * 2 + c)
        wac_in(q, 3).wait_recv()
        accumulate(q, xp(-3) * 2 + 1 - c)
        wac_in(q, 2).wait_recv()
        accumulate(q, xp(-2) * 2 + 1 - c)
        for b in range(16):
            grad_s[q, b] = grad[b * 32 : (b + 1) * 32, :].astype(BF16)
        for t in range(1, 16):
            grad_out(q, t).start()
        out_ref[:, q * 256 : q * 256 + 256] = grad[pl.ds(pl.multiple_of(mp * 32, 32), 32), :]

    for q in range(2):
        for t in range(1, 16):
            grad_in(q, t).wait_recv()
        acc = out_ref[:, q * 256 : q * 256 + 256]
        for t in range(1, 16):
            acc = acc + grad_r[q, lax.rem(mp + t, 16)].astype(F32)
        out_ref[:, q * 256 : q * 256 + 256] = acc

    for p in range(2):
        val_cp[p].wait_send()
        val_h2[p].wait_send()
        val_fw[p].wait_send()
    gain_cp.wait_send()
    w_far.wait_send()
    pow_cp.wait_send()
    for i in range(8):
        hid_out[i].wait_send()
        fwd_out[i].wait_send()
    for d in NEAR:
        wz_out(0, d).wait_send()
        wz_out(1, d).wait_send()
    for s in range(4):
        for u in range(2):
            ring_cp(0, s, u).wait_send()
            ring_cp(1, s, u).wait_send()
    for way in range(2):
        wx_out(way).wait_send()
        wx_fw(way).wait_send()
    for e in range(4):
        wc_out(e).wait_send()
        for q in range(2):
            wac_out(q, e).wait_send()
    nrm_out(x, 1 - c).wait_send()
    for e in range(1, 4):
        for q in range(2):
            wal_out(q, e).wait_send()
        for cc in range(2):
            nrm_out(xp(e), cc).wait_send()
    for d in range(1, 8):
        sq_out(d).wait_send()
    for q in range(2):
        for t in range(1, 16):
            grad_out(q, t).wait_send()


def per_device(
    teacher_hidden,
    teacher_gain,
    teacher_value,
    student_hidden,
    student_gain,
    student_value,
    segment_ids,
):
    vmem = pl.BlockSpec(memory_space=pltpu.VMEM)
    dma = pltpu.SemaphoreType.DMA
    return pl.pallas_call(
        kernel,
        out_shape=jax.ShapeDtypeStruct((32, 512), F32),
        in_specs=[pl.BlockSpec(memory_space=pl.ANY)] + [vmem] * 6,
        out_specs=vmem,
        scratch_shapes=[
            pltpu.VMEM((2048, 512), BF16),
            pltpu.VMEM((2048, 512), BF16),
            pltpu.VMEM((512, 512), BF16),
            pltpu.VMEM((256, 512), BF16),
            pltpu.VMEM((512,), BF16),
            pltpu.VMEM((8, 256, 512), BF16),
            pltpu.VMEM((8, 256, 512), BF16),
            pltpu.VMEM((8, 2, 256, 512), BF16),
            pltpu.VMEM((2, 4, 256, 512), BF16),
            pltpu.VMEM((2, 4, 256, 512), BF16),
            pltpu.VMEM((8, 8, 128), F32),
            pltpu.VMEM((8, 8, 128), F32),
            pltpu.VMEM((256, 512), F32),
            pltpu.VMEM((256, 512), F32),
            pltpu.VMEM((8, 128), F32),
            pltpu.VMEM((8, 128), F32),
            pltpu.VMEM((8, 1024), F32),
            pltpu.VMEM((2, 8, 256, 256), BF16),
            pltpu.VMEM((512, 256), F32),
            pltpu.VMEM((2, 16, 32, 256), BF16),
            pltpu.VMEM((2, 16, 32, 256), BF16),
            dma((3,)),
            dma((8,)),
            dma((8,)),
            dma((8,)),
            dma((8,)),
            dma((5,)),
            dma((5,)),
            dma((3, 2)),
            dma((3, 2)),
            dma((2, 8)),
            dma((2, 8)),
            dma((4,)),
            dma((4,)),
            dma((4,)),
            dma((4,)),
            dma((8,)),
            dma((8,)),
            dma((2, 4, 2)),
            dma((2, 4, 2)),
            dma((8,)),
            dma((8,)),
            dma((2, 3)),
            dma((2, 3)),
            dma((2, 4)),
            dma((2, 4)),
            dma((2, 16)),
            dma((2, 16)),
        ],
        compiler_params=pltpu.CompilerParams(
            collective_id=0, has_side_effects=True, vmem_limit_bytes=56 * 1024 * 1024
        ),
    )(
        teacher_hidden,
        teacher_gain,
        teacher_value,
        student_hidden,
        student_gain,
        student_value,
        segment_ids,
    )


def solution(mesh):
    return jax.shard_map(
        per_device,
        mesh=mesh,
        in_specs=(
            P("dp", "mp"),
            P("mp"),
            P("mp", "grp"),
            P(("dp", "mp"), None),
            P(),
            P(("dp", "mp"), "grp"),
            P("dp", None),
        ),
        out_specs=P(("dp", "mp"), "grp"),
        check_vma=False,
    )
```

time: 110 us -> 87.6 us (0.80)
  Pallas kernels: 105 us -> 85.5 us
  other arithmetic: 2.55 us -> 0 us
    pallas_call x1, Pallas kernels: 105 us -> 85.5 us  [per_device(): pl.pallas_call(kernel, out_shape=jax.ShapeDtypeStruct((32, 512), F32), in...]
    reshape x2 -> x0, other arithmetic: 2.55 us -> none  [the longest x1 1.3 us: per_device(): student_gain.astype(F32).reshape(1, -1)]
where the time goes in v2:
time: 87.6 us; the launch traced here: 87 us
  Pallas kernels  85.5 us (98%)
  local copies, waits for them, and re-layouts  1.47 us (2%)
    pallas_call x1, Pallas kernels, per_device(): pl.pallas_call(kernel, out_shape=jax.ShapeDtypeStruct((32, 512), F32), in...  85.5 us

profile of v2, /device:TPU:8, one launch (start us, length us, event | category | flops | bytes accessed | tf_op | source)
XLA Modules:
  0.0 87.0 jit_solution(7186793565905151359)
XLA Ops:
  0.0 85.5 %shard_map.73 = f32[32,512]{1,0:T(8,128)} custom-call(bf16[4096,512]{1,0:T(8,128)(2,1)} %hid_ref.1, bf16[512]{0:T(512)(128)(2,1)} %gain_ref.1, bf16[512,512]{1,0:T(8,128)(2,1)} %val_ref.1, bf16[256,4096]{1,0:T(8,128)(2,1)} %stu_ref.1, bf16[4096]{0:T(1024)(128)(2,1)} %sgain_ref.1, bf16[32,512]{1,0:T(8,128)(2,1)} %wsh_ref.1, s32[4,1024]{1,0:T(4,128)} %seg_ref.1), custom_call_target="tpu_custom_call" | custom-call | tf_op jit(solution)/shard_map/pallas_call | solution.py:565
  85.5 1.5 %copy.9 = f32[32,512]{1,0:T(8,128)} copy(f32[32,512]{1,0:T(8,128)} %shard_map.73) | data formatting | bytes 131072

commit v3 on v2

--- a/solution.py
+++ b/solution.py
@@ -17,6 +17,8 @@
 power_eps = 1e-06
 
 ORDER = (4, 3, -3, 2, -2, 1, -1, 0)
+NQ = 4
+QW = 512 // NQ
 NEAR = (4, 3, -3, 2, -2, 1, -1)
 
 
@@ -32,10 +34,10 @@
     own,
     oth,
     valo,
-    valt,
     gaino,
     nrm,
     nall,
+    nturn,
     wgt,
     ring_s,
     ring_r,
@@ -57,8 +59,10 @@
     fwd_rs,
     misc_ss,
     misc_rs,
-    val_ss,
-    val_rs,
+    vx_ss,
+    vx_rs,
+    vc_ss,
+    vc_rs,
     wz_ss,
     wz_rs,
     wx_ss,
@@ -67,6 +71,8 @@
     wc_rs,
     nrm_ss,
     nrm_rs,
+    swap_ss,
+    swap_rs,
     ring_ss,
     ring_rs,
     sq_ss,
@@ -179,21 +185,34 @@
     w_far = rc(wsh_ref, wrow(h), misc_ss.at[3], misc_rs.at[3], far_dev)
     w_far_in = rc(wsh_ref, wrow(1 - h), misc_ss.at[3], misc_rs.at[3], far_dev)
     w_far.start()
-    hop1_dev = at(grp=1 - g, hh=(1 - h) * (1 - c) + h * c)
-    hop2_dev = at(grp=1 - g, hh=h * (1 - c) + (1 - h) * c)
-
-    def vrows(cc, p):
-        return pl.ds(pl.multiple_of(cc * 256 + p * 128, 128), 128)
-
-    val_cp, val_h2, val_fw, val_in = [], [], [], []
-    for p in range(2):
-        tmp = valt.at[pl.ds(p * 128, 128), :]
-        mine, theirs = valo.at[vrows(c, p), :], valo.at[vrows(1 - c, p), :]
-        val_cp.append(rc(val_ref.at[vrows(c, p), :], tmp, val_ss.at[0, p], val_rs.at[0, p], hop1_dev))
-        val_h2.append(rc(tmp, mine, val_ss.at[1, p], val_rs.at[1, p], hop2_dev))
-        val_fw.append(rc(mine, mine, val_ss.at[2, p], val_rs.at[2, p], core_dev))
-        val_in.append(rc(theirs, theirs, val_ss.at[2, p], val_rs.at[2, p], core_dev))
-        val_cp[p].start()
+    def vblock(xx, cc):
+        return valo.at[pl.ds(pl.multiple_of((xx * 2 + cc) * 64, 64), 64), :]
+
+    val_cp = rc(
+        val_ref.at[pl.ds(pl.multiple_of(dp * 64, 64), 64), :],
+        vblock(x, c),
+        misc_ss.at[0],
+        misc_rs.at[0],
+        far_dev,
+    )
+    val_cp.start()
+
+    def vx_out(e):
+        b = vblock(x, c)
+        return rc(b, b, vx_ss.at[e], vx_rs.at[e], at(xx=xp(e)))
+
+    def vx_in(e):
+        b = vblock(xp(-e), c)
+        return rc(b, b, vx_ss.at[e], vx_rs.at[e], at(xx=xp(e)))
+
+    def vc_out(e):
+        b = vblock(xp(-e), c)
+        return rc(b, b, vc_ss.at[e], vc_rs.at[e], core_dev)
+
+    def vc_in(e):
+        b = vblock(xp(-e), 1 - c)
+        return rc(b, b, vc_ss.at[e], vc_rs.at[e], core_dev)
+
     gain_cp = rc(gain_ref, gaino, misc_ss.at[2], misc_rs.at[2], cross_dev)
     gain_cp.start()
 
@@ -221,7 +240,8 @@
         fwd_in.append(rc(theirs, theirs, fwd_ss.at[i], fwd_rs.at[i], grp_dev))
     for d in NEAR:
         wz_out(0, d).start()
-    hid_out[0].start()
+    for i in range(8):
+        hid_out[i].start()
 
     def nrm_out(xx, cc):
         to = xx * 2 + cc
@@ -231,11 +251,33 @@
         fr = xx * 2 + cc
         return rc(nall.at[fr], nall.at[fr], nrm_ss.at[fr], nrm_rs.at[fr], at(xx=xx, cc=cc))
 
+    grows = lambda gg: pl.ds(pl.multiple_of(gg * 128, 128), 128)
+
+    def far_out(cc):
+        to = xp(2) * 2 + cc
+        return rc(
+            nrm.at[to, grows(g), :],
+            nall.at[dp, grows(g), :],
+            nrm_ss.at[to],
+            nrm_rs.at[dp],
+            at(xx=xp(2), cc=cc),
+        )
+
+    def far_in(cc):
+        b = nall.at[xp(2) * 2 + cc, grows(g), :]
+        return rc(b, b, nrm_ss.at[xp(2) * 2 + cc], nrm_rs.at[xp(2) * 2 + cc], grp_dev)
+
+    def swap_out(cc):
+        b = nall.at[xp(2) * 2 + cc, grows(g), :]
+        return rc(b, b, swap_ss.at[cc], swap_rs.at[cc], grp_dev)
+
+    def swap_in(cc):
+        b = nall.at[xp(2) * 2 + cc, grows(1 - g), :]
+        return rc(b, b, swap_ss.at[cc], swap_rs.at[cc], grp_dev)
+
     nrm_out(x, 1 - c).start()
     for e in (1, 3):
-        for cc in range(2):
-            nrm_out(xp(e), cc).start()
-    nrm_out(xp(2), c).start()
+        nrm_out(xp(e), c).start()
 
     def wblock(xx, cc=None):
         return wgt.at[xx * 2 + (c if cc is None else cc)]
@@ -243,20 +285,21 @@
     def wx_dev(way):
         return at(xx=xp(1 if way == 0 else -1))
 
-    def wx_out(way):
-        return rc(wblock(x), wblock(x), wx_ss.at[way], wx_rs.at[way], wx_dev(way))
-
-    def wx_in(way):
-        b = wblock(xp(-1 if way == 0 else 1))
-        return rc(b, b, wx_ss.at[way], wx_rs.at[way], wx_dev(way))
+    def wx_out(way, part):
+        b = wblock(x).at[way if part == 0 else 1 - way]
+        return rc(b, b, wx_ss.at[part, way], wx_rs.at[part, way], wx_dev(way))
+
+    def wx_in(way, part):
+        b = wblock(xp(-1 if way == 0 else 1)).at[way if part == 0 else 1 - way]
+        return rc(b, b, wx_ss.at[part, way], wx_rs.at[part, way], wx_dev(way))
 
     def wx_fw(way):
         b = wblock(xp(-1 if way == 0 else 1)).at[way]
-        return rc(b, b, wx_ss.at[2 + way], wx_rs.at[2 + way], wx_dev(way))
+        return rc(b, b, wx_ss.at[2, way], wx_rs.at[2, way], wx_dev(way))
 
     def wx_fin(way):
         b = wblock(xp(2)).at[way]
-        return rc(b, b, wx_ss.at[2 + way], wx_rs.at[2 + way], wx_dev(way))
+        return rc(b, b, wx_ss.at[2, way], wx_rs.at[2, way], wx_dev(way))
 
     def wc_out(e):
         b = wblock(xp(e))
@@ -331,11 +374,12 @@
         if u == 1 and d != 0:
             sq_out(d).start()
 
+    def turn(slot):
+        nturn[slot] = nall[slot].T
+
     def take(i):
         hid_in[i].wait_recv()
         fwd_out[i].start()
-        if i + 3 < 8:
-            hid_out[i + 3].start()
 
     def add_states(blocks):
         part = None
@@ -348,69 +392,84 @@
         states[...] += part
 
     states[...] = jnp.zeros_like(states)
+    val_cp.wait_recv()
+    for e in (1, 3, 2):
+        vx_out(e).start()
+    vc_out(0).start()
+    for e in (1, 3):
+        nrm_out(xp(e), 1 - c).start()
     w_far_in.wait_recv()
     for d in NEAR:
         wz_out(1, d).start()
-    for p in range(2):
-        val_cp[p].wait_recv()
-        val_h2[p].start()
-    hid_out[1].start()
-    hid_out[2].start()
     take(0)
-    for p in range(2):
-        val_h2[p].wait_recv()
-        val_fw[p].start()
+    for e in (1, 3, 2):
+        vx_in(e).wait_recv()
+        vc_out(e).start()
     own_cp.wait()
     w_cp.wait()
     gain_cp.wait_recv()
-    for p in range(2):
-        val_in[p].wait_recv()
+    take(1)
+    for e in range(4):
+        vc_in(e).wait_recv()
     sub(0, 0)
+    sub(0, 1)
     for b in range(2):
         for d in NEAR:
             wz_in(b, d).wait_recv()
-    wx_out(0).start()
-    wx_out(1).start()
+    for part in range(2):
+        for way in range(2):
+            wx_out(way, part).start()
     wc_out(0).start()
-    take(1)
     take(2)
-    sub(0, 1)
     sub(1, 0)
     sub(2, 0)
     take(3)
+    nrm_own.wait()
+    turn(dp)
+    nrm_in(x, 1 - c).wait_recv()
+    turn(x * 2 + 1 - c)
     sub(1, 1)
     sub(2, 1)
     take(4)
     sub(3, 0)
     sub(4, 0)
     for way in range(2):
-        wx_in(way).wait_recv()
+        wx_in(way, 0).wait_recv()
         wx_fw(way).start()
-    wc_out(1).start()
-    wc_out(3).start()
+    for cc in range(2):
+        far_out(cc).start()
     take(5)
     sub(3, 1)
     sub(4, 1)
+    for cc in range(2):
+        nrm_in(xp(1), cc).wait_recv()
+        turn(xp(1) * 2 + cc)
     take(6)
-    add_states((xp(1) * 2 + c, xp(-1) * 2 + c))
     wc_in(0).wait_recv()
     add_states((dp, x * 2 + 1 - c))
     sub(5, 0)
     sub(6, 0)
+    for way in range(2):
+        wx_in(way, 1).wait_recv()
+    wc_out(1).start()
+    wc_out(3).start()
+    add_states((xp(1) * 2 + c, xp(-1) * 2 + c))
     take(7)
     sub(5, 1)
     sub(6, 1)
+    for cc in range(2):
+        nrm_in(xp(3), cc).wait_recv()
+        turn(xp(3) * 2 + cc)
+    wc_in(1).wait_recv()
+    wc_in(3).wait_recv()
+    add_states((xp(1) * 2 + 1 - c, xp(-1) * 2 + 1 - c))
     wx_fin(0).wait_recv()
     wx_fin(1).wait_recv()
     wc_out(2).start()
-    nrm_out(xp(2), 1 - c).start()
-    wc_in(1).wait_recv()
-    wc_in(3).wait_recv()
-    add_states((xp(1) * 2 + 1 - c, xp(-1) * 2 + 1 - c))
     sub(7, 0)
-    sub(7, 1)
     wc_in(2).wait_recv()
     add_states((xp(2) * 2, xp(2) * 2 + 1))
+    sub(7, 1)
 
     for d in range(1, 8):
         sq_in(d).wait_recv()
@@ -455,69 +514,72 @@
             grad_r.at[q, fr], grad_r.at[q, fr], grad_ss.at[q, fr], grad_rs.at[q, fr], (g, dp, fr)
         )
 
+    for cc in range(2):
+        far_in(cc).wait_recv()
+        swap_out(cc).start()
     pow_cp.wait_recv()
     divs = []
     for j in range(2):
         power = (pow_s[j : j + 1, :] + pow_r[j : j + 1, :]) / KV + power_eps
         length = len_row[0:1, pl.ds(pl.multiple_of((mp % 4) * 256 + j * 128, 128), 128)]
         divs.append(to_col(length * power))
-    for q in range(2):
+    for q in range(NQ):
         for j in range(2):
             rows = slice(j * 128, (j + 1) * 128)
-            wall[q, dp, rows, :] = (total[rows, q * 256 : q * 256 + 256] / divs[j]).astype(BF16)
+            wall[q, dp, rows, :] = (total[rows, q * QW : q * QW + QW] / divs[j]).astype(BF16)
         for e in (1, 3, 2):
             wal_out(q, e).start()
         wac_out(q, 0).start()
 
-    nrm_own.wait()
-    nrm_in(x, 1 - c).wait_recv()
-    for e in (1, 3, 2):
-        for cc in range(2):
-            nrm_in(xp(-e), cc).wait_recv()
-
     def accumulate(q, slot):
-        grad[...] += lax.dot_general(
-            nall[slot], wall[q, slot], (((0,), (0,)), ((), ())), preferred_element_type=F32
-        )
-
-    for q in range(2):
-        grad[...] = jnp.zeros_like(grad)
+        grad[q % 2] += jnp.dot(nturn[slot], wall[q, slot], preferred_element_type=F32)
+
+    def begin(q):
+        grad[q % 2] = jnp.zeros((512, QW), F32)
         accumulate(q, dp)
         wac_in(q, 0).wait_recv()
         accumulate(q, x * 2 + 1 - c)
-        wal_in(q, 1).wait_recv()
-        wac_out(q, 1).start()
+
+    begin(0)
+    for q in range(NQ):
+        for e in (1, 3):
+            wal_in(q, e).wait_recv()
+            wac_out(q, e).start()
         accumulate(q, xp(-1) * 2 + c)
-        wal_in(q, 3).wait_recv()
-        wac_out(q, 3).start()
         accumulate(q, xp(-3) * 2 + c)
-        wac_in(q, 1).wait_recv()
-        accumulate(q, xp(-1) * 2 + 1 - c)
+        if q == 0:
+            for cc in range(2):
+                swap_in(cc).wait_recv()
+                turn(xp(2) * 2 + cc)
         wal_in(q, 2).wait_recv()
         wac_out(q, 2).start()
         accumulate(q, xp(-2) * 2 + c)
-        wac_in(q, 3).wait_recv()
-        accumulate(q, xp(-3) * 2 + 1 - c)
+        for e in (1, 3):
+            wac_in(q, e).wait_recv()
+            accumulate(q, xp(-e) * 2 + 1 - c)
+        if q + 1 < NQ:
+            begin(q + 1)
         wac_in(q, 2).wait_recv()
         accumulate(q, xp(-2) * 2 + 1 - c)
         for b in range(16):
-            grad_s[q, b] = grad[b * 32 : (b + 1) * 32, :].astype(BF16)
+            grad_s[q, b] = grad[q % 2, b * 32 : (b + 1) * 32, :].astype(BF16)
         for t in range(1, 16):
             grad_out(q, t).start()
-        out_ref[:, q * 256 : q * 256 + 256] = grad[pl.ds(pl.multiple_of(mp * 32, 32), 32), :]
-
-    for q in range(2):
+        out_ref[:, q * QW : q * QW + QW] = grad[q % 2, pl.ds(pl.multiple_of(mp * 32, 32), 32), :]
+
+    for q in range(NQ):
         for t in range(1, 16):
             grad_in(q, t).wait_recv()
-        acc = out_ref[:, q * 256 : q * 256 + 256]
+        acc = out_ref[:, q * QW : q * QW + QW]
         for t in range(1, 16):
             acc = acc + grad_r[q, lax.rem(mp + t, 16)].astype(F32)
-        out_ref[:, q * 256 : q * 256 + 256] = acc
-
-    for p in range(2):
-        val_cp[p].wait_send()
-        val_h2[p].wait_send()
-        val_fw[p].wait_send()
+        out_ref[:, q * QW : q * QW + QW] = acc
+
+    val_cp.wait_send()
+    for e in range(4):
+        if e > 0:
+            vx_out(e).wait_send()
+        vc_out(e).wait_send()
     gain_cp.wait_send()
     w_far.wait_send()
     pow_cp.wait_send()
@@ -532,21 +594,24 @@
             ring_cp(0, s, u).wait_send()
             ring_cp(1, s, u).wait_send()
     for way in range(2):
-        wx_out(way).wait_send()
+        wx_out(way, 0).wait_send()
+        wx_out(way, 1).wait_send()
         wx_fw(way).wait_send()
     for e in range(4):
         wc_out(e).wait_send()
-        for q in range(2):
+        for q in range(NQ):
             wac_out(q, e).wait_send()
     nrm_out(x, 1 - c).wait_send()
+    for cc in range(2):
+        swap_out(cc).wait_send()
     for e in range(1, 4):
-        for q in range(2):
+        for q in range(NQ):
             wal_out(q, e).wait_send()
         for cc in range(2):
-            nrm_out(xp(e), cc).wait_send()
+            (nrm_out(xp(e), cc) if e != 2 else far_out(cc)).wait_send()
     for d in range(1, 8):
         sq_out(d).wait_send()
-    for q in range(2):
+    for q in range(NQ):
         for t in range(1, 16):
             grad_out(q, t).wait_send()
 
@@ -571,10 +636,10 @@
             pltpu.VMEM((2048, 512), BF16),
             pltpu.VMEM((2048, 512), BF16),
             pltpu.VMEM((512, 512), BF16),
-            pltpu.VMEM((256, 512), BF16),
             pltpu.VMEM((512,), BF16),
             pltpu.VMEM((8, 256, 512), BF16),
             pltpu.VMEM((8, 256, 512), BF16),
+            pltpu.VMEM((8, 512, 256), BF16),
             pltpu.VMEM((8, 2, 256, 512), BF16),
             pltpu.VMEM((2, 4, 256, 512), BF16),
             pltpu.VMEM((2, 4, 256, 512), BF16),
@@ -585,10 +650,10 @@
             pltpu.VMEM((8, 128), F32),
             pltpu.VMEM((8, 128), F32),
             pltpu.VMEM((8, 1024), F32),
-            pltpu.VMEM((2, 8, 256, 256), BF16),
-            pltpu.VMEM((512, 256), F32),
-            pltpu.VMEM((2, 16, 32, 256), BF16),
-            pltpu.VMEM((2, 16, 32, 256), BF16),
+            pltpu.VMEM((NQ, 8, 256, QW), BF16),
+            pltpu.VMEM((2, 512, QW), F32),
+            pltpu.VMEM((NQ, 16, 32, QW), BF16),
+            pltpu.VMEM((NQ, 16, 32, QW), BF16),
             dma((3,)),
             dma((8,)),
             dma((8,)),
@@ -596,26 +661,30 @@
             dma((8,)),
             dma((5,)),
             dma((5,)),
-            dma((3, 2)),
-            dma((3, 2)),
-            dma((2, 8)),
-            dma((2, 8)),
             dma((4,)),
             dma((4,)),
             dma((4,)),
             dma((4,)),
+            dma((2, 8)),
+            dma((2, 8)),
+            dma((3, 2)),
+            dma((3, 2)),
+            dma((4,)),
+            dma((4,)),
             dma((8,)),
             dma((8,)),
+            dma((2,)),
+            dma((2,)),
             dma((2, 4, 2)),
             dma((2, 4, 2)),
             dma((8,)),
             dma((8,)),
-            dma((2, 3)),
-            dma((2, 3)),
-            dma((2, 4)),
-            dma((2, 4)),
-            dma((2, 16)),
-            dma((2, 16)),
+            dma((NQ, 3)),
+            dma((NQ, 3)),
+            dma((NQ, 4)),
+            dma((NQ, 4)),
+            dma((NQ, 16)),
+            dma((NQ, 16)),
         ],
         compiler_params=pltpu.CompilerParams(
             collective_id=0, has_side_effects=True, vmem_limit_bytes=56 * 1024 * 1024

time: 87.6 us -> 81.3 us (0.928)
  Pallas kernels: 85.5 us -> 78.8 us
    pallas_call x1, Pallas kernels: 85.5 us -> 78.8 us  [per_device(): pl.pallas_call(kernel, out_shape=jax.ShapeDtypeStruct((32, 512), F32), in...]
where the time goes in v3:
time: 81.3 us; the launch traced here: 80.2 us
  Pallas kernels  78.8 us (97%)
  local copies, waits for them, and re-layouts  1.47 us (2%)
    pallas_call x1, Pallas kernels, per_device(): pl.pallas_call(kernel, out_shape=jax.ShapeDtypeStruct((32, 512), F32), in...  78.8 us

profile of v3, /device:TPU:8, one launch (start us, length us, event | category | flops | bytes accessed | tf_op | source)
XLA Modules:
  0.0 80.2 jit_solution(12723116567296520105)
XLA Ops:
  0.0 78.8 %shard_map.73 = f32[32,512]{1,0:T(8,128)} custom-call(bf16[4096,512]{1,0:T(8,128)(2,1)} %hid_ref.1, bf16[512]{0:T(512)(128)(2,1)} %gain_ref.1, bf16[512,512]{1,0:T(8,128)(2,1)} %val_ref.1, bf16[256,4096]{1,0:T(8,128)(2,1)} %stu_ref.1, bf16[4096]{0:T(1024)(128)(2,1)} %sgain_ref.1, bf16[32,512]{1,0:T(8,128)(2,1)} %wsh_ref.1, s32[4,1024]{1,0:T(4,128)} %seg_ref.1), custom_call_target="tpu_custom_call" | custom-call | tf_op jit(solution)/shard_map/pallas_call | solution.py:630
  78.8 1.5 %copy.9 = f32[32,512]{1,0:T(8,128)} copy(f32[32,512]{1,0:T(8,128)} %shard_map.73) | data formatting | bytes 131072

commit v4 on v3

--- a/solution.py
+++ b/solution.py
@@ -17,6 +17,7 @@
 power_eps = 1e-06
 
 ORDER = (4, 3, -3, 2, -2, 1, -1, 0)
+NHID = 2
 NQ = 4
 QW = 512 // NQ
 NEAR = (4, 3, -3, 2, -2, 1, -1)
@@ -24,13 +25,18 @@
 
 def kernel(
     hid_ref,
+    gain_in,
+    val_in,
+    stu_in,
+    sgain_in,
+    wsh_ref,
+    seg_in,
+    out_ref,
     gain_ref,
     val_ref,
     stu_ref,
     sgain_ref,
-    wsh_ref,
     seg_ref,
-    out_ref,
     own,
     oth,
     valo,
@@ -73,6 +79,8 @@
     nrm_rs,
     swap_ss,
     swap_rs,
+    pow_ss,
+    pow_rs,
     ring_ss,
     ring_rs,
     sq_ss,
@@ -112,11 +120,18 @@
     own_cp = pltpu.make_async_copy(
         hid_ref.at[pl.ds(pl.multiple_of(h * 2048, 2048), 2048), :], own, loc_sem.at[0]
     )
-    own_cp.start()
     w_cp = pltpu.make_async_copy(
         wsh_ref, wgt.at[dp, h, pl.ds(pl.multiple_of(z * 32, 32), 32), :], loc_sem.at[1]
     )
     w_cp.start()
+    gain_ld = pltpu.make_async_copy(gain_in, gain_ref, loc_sem.at[3])
+    val_ld = pltpu.make_async_copy(val_in, val_ref, loc_sem.at[4])
+    stu_ld = pltpu.make_async_copy(stu_in, stu_ref, loc_sem.at[5])
+    sgain_ld = pltpu.make_async_copy(sgain_in, sgain_ref, loc_sem.at[6])
+    seg_ld = pltpu.make_async_copy(seg_in, seg_ref, loc_sem.at[7])
+    for ld in (stu_ld, sgain_ld, seg_ld, gain_ld, val_ld):
+        ld.start()
+    own_cp.start()
 
     barrier = pltpu.get_barrier_semaphore()
     count = 0
@@ -136,37 +151,6 @@
         pl.semaphore_signal(barrier, inc=1, device_id=dev, device_id_type=MESH)
         count += 1
 
-    sgain = sgain_ref[...].astype(F32).reshape(1, DS)
-
-    @pl.loop(0, 8)
-    def _(i):
-        rows = pl.ds(pl.multiple_of(i * 32, 32), 32)
-        wide = stu_ref[rows, :].astype(F32)
-        scale = lax.rsqrt(jnp.sum(wide * wide, axis=1, keepdims=True) / DS + norm_eps)
-        done = (wide * scale * sgain).astype(BF16)
-        for b in range(8):
-            nrm[b, rows, :] = done[:, b * 512 : (b + 1) * 512]
-
-    nrm_own = pltpu.make_async_copy(nrm.at[dp], nall.at[dp], loc_sem.at[2])
-    nrm_own.start()
-
-    seg = seg_ref[pl.ds(mp // 4, 1), :]
-    lens = jnp.zeros((1, 1024), F32)
-    for s in range(NSEG):
-        hit = (seg == s).astype(F32)
-        lens = lens + hit * jnp.sum(hit, axis=1, keepdims=True)
-    len_row[0:1, :] = lens
-
-    eye = lax.broadcasted_iota(jnp.int32, (128, 128), 0) == lax.broadcasted_iota(
-        jnp.int32, (128, 128), 1
-    )
-
-    def to_row(col):
-        return jnp.sum(jnp.where(eye, col, 0.0), axis=0, keepdims=True)
-
-    def to_col(row):
-        return jnp.sum(jnp.where(eye, row, 0.0), axis=1, keepdims=True)
-
     pl.semaphore_wait(barrier, count)
 
     def wz_piece(hh, d):
@@ -189,7 +173,7 @@
         return valo.at[pl.ds(pl.multiple_of((xx * 2 + cc) * 64, 64), 64), :]
 
     val_cp = rc(
-        val_ref.at[pl.ds(pl.multiple_of(dp * 64, 64), 64), :],
+        val_in.at[pl.ds(pl.multiple_of(dp * 64, 64), 64), :],
         vblock(x, c),
         misc_ss.at[0],
         misc_rs.at[0],
@@ -213,7 +197,7 @@
         b = vblock(xp(-e), 1 - c)
         return rc(b, b, vc_ss.at[e], vc_rs.at[e], core_dev)
 
-    gain_cp = rc(gain_ref, gaino, misc_ss.at[2], misc_rs.at[2], cross_dev)
+    gain_cp = rc(gain_in, gaino, misc_ss.at[2], misc_rs.at[2], cross_dev)
     gain_cp.start()
 
     def hid_rows(hh, i, j):
@@ -240,16 +224,24 @@
         fwd_in.append(rc(theirs, theirs, fwd_ss.at[i], fwd_rs.at[i], grp_dev))
     for d in NEAR:
         wz_out(0, d).start()
-    for i in range(8):
+    for i in range(NHID):
         hid_out[i].start()
 
-    def nrm_out(xx, cc):
-        to = xx * 2 + cc
-        return rc(nrm.at[to], nall.at[dp], nrm_ss.at[to], nrm_rs.at[dp], at(xx=xx, cc=cc))
-
-    def nrm_in(xx, cc):
+    def nrm_out(xx, cc, part):
+        to, rows = xx * 2 + cc, pl.ds(part * 128, 128)
+        return rc(
+            nrm.at[to, rows, :],
+            nall.at[dp, rows, :],
+            nrm_ss.at[to, part],
+            nrm_rs.at[dp, part],
+            at(xx=xx, cc=cc),
+        )
+
+    def nrm_wait(xx, cc):
         fr = xx * 2 + cc
-        return rc(nall.at[fr], nall.at[fr], nrm_ss.at[fr], nrm_rs.at[fr], at(xx=xx, cc=cc))
+        for part in range(2):
+            b = nall.at[fr, pl.ds(part * 128, 128), :]
+            rc(b, b, nrm_ss.at[fr, part], nrm_rs.at[fr, part], at(xx=xx, cc=cc)).wait_recv()
 
     grows = lambda gg: pl.ds(pl.multiple_of(gg * 128, 128), 128)
 
@@ -258,14 +250,14 @@
         return rc(
             nrm.at[to, grows(g), :],
             nall.at[dp, grows(g), :],
-            nrm_ss.at[to],
-            nrm_rs.at[dp],
+            nrm_ss.at[to, 0],
+            nrm_rs.at[dp, 0],
             at(xx=xp(2), cc=cc),
         )
 
     def far_in(cc):
         b = nall.at[xp(2) * 2 + cc, grows(g), :]
-        return rc(b, b, nrm_ss.at[xp(2) * 2 + cc], nrm_rs.at[xp(2) * 2 + cc], grp_dev)
+        return rc(b, b, nrm_ss.at[xp(2) * 2 + cc, 0], nrm_rs.at[xp(2) * 2 + cc, 0], grp_dev)
 
     def swap_out(cc):
         b = nall.at[xp(2) * 2 + cc, grows(g), :]
@@ -275,9 +267,44 @@
         b = nall.at[xp(2) * 2 + cc, grows(1 - g), :]
         return rc(b, b, swap_ss.at[cc], swap_rs.at[cc], grp_dev)
 
-    nrm_out(x, 1 - c).start()
+    stu_ld.wait()
+    sgain_ld.wait()
+    sgain = sgain_ref[...].astype(F32).reshape(1, DS)
+
+    @pl.loop(0, 8)
+    def _(i):
+        rows = pl.ds(pl.multiple_of(i * 32, 32), 32)
+        wide = stu_ref[rows, :].astype(F32)
+        scale = lax.rsqrt(jnp.sum(wide * wide, axis=1, keepdims=True) / DS + norm_eps)
+        done = (wide * scale * sgain).astype(BF16)
+        for b in range(8):
+            nrm[b, rows, :] = done[:, b * 512 : (b + 1) * 512]
+
+    nrm_own = pltpu.make_async_copy(nrm.at[dp], nall.at[dp], loc_sem.at[2])
+    nrm_own.start()
+
+    seg_ld.wait()
+    seg = seg_ref[pl.ds(mp // 4, 1), :]
+    lens = jnp.zeros((1, 1024), F32)
+    for s in range(NSEG):
+        hit = (seg == s).astype(F32)
+        lens = lens + hit * jnp.sum(hit, axis=1, keepdims=True)
+    len_row[0:1, :] = lens
+
+    eye = lax.broadcasted_iota(jnp.int32, (128, 128), 0) == lax.broadcasted_iota(
+        jnp.int32, (128, 128), 1
+    )
+
+    def to_row(col):
+        return jnp.sum(jnp.where(eye, col, 0.0), axis=0, keepdims=True)
+
+    def to_col(row):
+        return jnp.sum(jnp.where(eye, row, 0.0), axis=1, keepdims=True)
+
     for e in (1, 3):
-        nrm_out(xp(e), c).start()
+        nrm_out(xp(e), c, 0).start()
+    for part in range(2):
+        nrm_out(x, 1 - c, part).start()
 
     def wblock(xx, cc=None):
         return wgt.at[xx * 2 + (c if cc is None else cc)]
@@ -309,8 +336,11 @@
         b = wblock(xp(e), 1 - c)
         return rc(b, b, wc_ss.at[e], wc_rs.at[e], core_dev)
 
+    jrow = lambda u: g if u == 0 else 1 - g
+    urows = lambda j: pl.ds(pl.multiple_of(j * 128, 128), 128)
+
     def ring_cp(way, s, u):
-        rows = pl.ds(pl.multiple_of((g if u == 0 else 1 - g) * 128, 128), 128)
+        rows = urows(jrow(u))
         cols = pl.ds(way * 256, 256) if s == 0 else pl.ds(0, 512)
         dev = at(zz=zp(1 if way == 0 else -1))
         return rc(
@@ -330,7 +360,7 @@
     def sub(i, u):
         d = ORDER[i]
         k = zp(d)
-        j = g if u == 0 else 1 - g
+        j = jrow(u)
         if u == 1:
             fwd_in[i].wait_recv()
         if d == 0:
@@ -339,13 +369,17 @@
         elif d != 4:
             ring_cp(0 if d > 0 else 1, 3 - abs(d), u).wait_recv()
         rows = pl.ds(pl.multiple_of(k * 256 + j * 128, 128), 128)
-        brows = pl.ds(pl.multiple_of(j * 128, 128), 128)
+        brows = urows(j)
         h1 = own[rows, :].astype(F32)
         h2 = oth[rows, :].astype(F32)
         tgain = gain_ref[...].astype(F32).reshape(1, 512)
         tgaino = gaino[...].astype(F32).reshape(1, 512)
         acc = jnp.dot((h1 * tgain).astype(BF16), val_ref[...], preferred_element_type=F32)
         acc += jnp.dot((h2 * tgaino).astype(BF16), valo[...], preferred_element_type=F32)
+        sq = jnp.sum(h1 * h1 + h2 * h2, axis=1, keepdims=True)
+        sq_s[k, pl.ds(j, 1), :] = to_row(sq)
+        if u == 1 and d != 0:
+            sq_out(d).start()
         if d == 4:
             ring_s[0, 0, brows, 0:256] = acc[:, 0:256].astype(BF16)
             ring_s[1, 0, brows, 256:512] = acc[:, 256:512].astype(BF16)
@@ -369,10 +403,6 @@
                     acc + ring_r[way, s - 1, brows, :].astype(F32)
                 ).astype(BF16)
             ring_cp(way, s, u).start()
-        sq = jnp.sum(h1 * h1 + h2 * h2, axis=1, keepdims=True)
-        sq_s[k, pl.ds(j, 1), :] = to_row(sq)
-        if u == 1 and d != 0:
-            sq_out(d).start()
 
     def turn(slot):
         nturn[slot] = nall[slot].T
@@ -393,11 +423,16 @@
 
     states[...] = jnp.zeros_like(states)
     val_cp.wait_recv()
-    for e in (1, 3, 2):
+    for e in (2, 1, 3):
         vx_out(e).start()
     vc_out(0).start()
     for e in (1, 3):
-        nrm_out(xp(e), 1 - c).start()
+        nrm_out(xp(e), c, 1).start()
+    for part in range(2):
+        for e in (1, 3):
+            nrm_out(xp(e), 1 - c, part).start()
+    for i in range(NHID, 8):
+        hid_out[i].start()
     w_far_in.wait_recv()
     for d in NEAR:
         wz_out(1, d).start()
@@ -407,6 +442,8 @@
         vc_out(e).start()
     own_cp.wait()
     w_cp.wait()
+    gain_ld.wait()
+    val_ld.wait()
     gain_cp.wait_recv()
     take(1)
     for e in range(4):
@@ -426,81 +463,91 @@
     take(3)
     nrm_own.wait()
     turn(dp)
-    nrm_in(x, 1 - c).wait_recv()
+    nrm_wait(x, 1 - c)
     turn(x * 2 + 1 - c)
     sub(1, 1)
     sub(2, 1)
     take(4)
     sub(3, 0)
     sub(4, 0)
+    take(5)
+    sub(3, 1)
+    sub(4, 1)
     for way in range(2):
         wx_in(way, 0).wait_recv()
         wx_fw(way).start()
     for cc in range(2):
-        far_out(cc).start()
-    take(5)
-    sub(3, 1)
-    sub(4, 1)
-    for cc in range(2):
-        nrm_in(xp(1), cc).wait_recv()
+        nrm_wait(xp(1), cc)
         turn(xp(1) * 2 + cc)
     take(6)
     wc_in(0).wait_recv()
     add_states((dp, x * 2 + 1 - c))
     sub(5, 0)
     sub(6, 0)
+    take(7)
+    sub(5, 1)
+    sub(6, 1)
+    for cc in range(2):
+        far_out(cc).start()
     for way in range(2):
         wx_in(way, 1).wait_recv()
     wc_out(1).start()
     wc_out(3).start()
     add_states((xp(1) * 2 + c, xp(-1) * 2 + c))
-    take(7)
-    sub(5, 1)
-    sub(6, 1)
     for cc in range(2):
-        nrm_in(xp(3), cc).wait_recv()
+        nrm_wait(xp(3), cc)
         turn(xp(3) * 2 + cc)
+    def power(j):
+        rows = urows(j)
+        row = sq_s[z, pl.ds(j, 1), :]
+        for d in range(1, 8):
+            row = row + sq_r[zp(d), pl.ds(j, 1), :]
+        target = total[rows, :] * lax.rsqrt(to_col(row) / DT + norm_eps)
+        total[rows, :] = target
+        pow_s[j, 0:1, :] = to_row(jnp.sum(target * target, axis=1, keepdims=True))
+        pow_cp(j).start()
+
+    def pow_cp(j):
+        return rc(pow_s.at[j], pow_r.at[j], pow_ss.at[j], pow_rs.at[j], grp_dev)
+
+    sub(7, 0)
+    for d in range(1, 8):
+        sq_in(d).wait_recv()
+    power(g)
+    wx_fin(0).wait_recv()
+    wx_fin(1).wait_recv()
+    wc_out(2).start()
+    sub(7, 1)
+    power(1 - g)
     wc_in(1).wait_recv()
     wc_in(3).wait_recv()
     add_states((xp(1) * 2 + 1 - c, xp(-1) * 2 + 1 - c))
-    wx_fin(0).wait_recv()
-    wx_fin(1).wait_recv()
-    wc_out(2).start()
-    sub(7, 0)
+    far_in(c).wait_recv()
+    swap_out(c).start()
     wc_in(2).wait_recv()
     add_states((xp(2) * 2, xp(2) * 2 + 1))
-    sub(7, 1)
-
-    for d in range(1, 8):
-        sq_in(d).wait_recv()
-    sq_r[z] = sq_s[z]
-    rows_sq = jnp.zeros((8, 128), F32)
-    for s in range(8):
-        rows_sq = rows_sq + sq_r[s]
-    for j in range(2):
-        rows = slice(j * 128, (j + 1) * 128)
-        scale = lax.rsqrt(to_col(rows_sq[j : j + 1, :]) / DT + norm_eps)
-        target = total[rows, :] * scale
-        total[rows, :] = states[rows, :] - target
-        pow_s[j : j + 1, :] = to_row(jnp.sum(target * target, axis=1, keepdims=True))
-    pow_cp = rc(pow_s, pow_r, misc_ss.at[4], misc_rs.at[4], grp_dev)
-    pow_cp.start()
-
-    def wal_out(q, e):
-        b = wall.at[q, dp]
-        return rc(b, b, wal_ss.at[q, e - 1], wal_rs.at[q, e - 1], at(xx=xp(e)))
-
-    def wal_in(q, e):
-        b = wall.at[q, xp(-e) * 2 + c]
-        return rc(b, b, wal_ss.at[q, e - 1], wal_rs.at[q, e - 1], at(xx=xp(e)))
-
-    def wac_out(q, e):
-        b = wall.at[q, xp(-e) * 2 + c]
-        return rc(b, b, wac_ss.at[q, e], wac_rs.at[q, e], core_dev)
-
-    def wac_in(q, e):
-        b = wall.at[q, xp(-e) * 2 + 1 - c]
-        return rc(b, b, wac_ss.at[q, e], wac_rs.at[q, e], core_dev)
+
+    def wal_out(q, e, u):
+        b = wall.at[q, dp, urows(u), :]
+        return rc(b, b, wal_ss.at[q, e - 1, u], wal_rs.at[q, e - 1, u], at(xx=xp(e)))
+
+    def wal_in(q, e, u):
+        b = wall.at[q, xp(-e) * 2 + c, urows(u), :]
+        return rc(b, b, wal_ss.at[q, e - 1, u], wal_rs.at[q, e - 1, u], at(xx=xp(e)))
+
+    def wac_out(q, e, u):
+        b = wall.at[q, xp(-e) * 2 + c, urows(u), :]
+        return rc(b, b, wac_ss.at[q, e, u], wac_rs.at[q, e, u], core_dev)
+
+    def wac_wait(q, e):
+        for u in range(2):
+            b = wall.at[q, xp(-e) * 2 + 1 - c, urows(u), :]
+            rc(b, b, wac_ss.at[q, e, u], wac_rs.at[q, e, u], core_dev).wait_recv()
+
+    def pass_on(q, e):
+        for j in (1 - g, g):
+            wal_in(q, e, j).wait_recv()
+            wac_out(q, e, j).start()
 
     def grad_out(q, t):
         to = lax.rem(mp + t, 16)
@@ -514,22 +561,25 @@
             grad_r.at[q, fr], grad_r.at[q, fr], grad_ss.at[q, fr], grad_rs.at[q, fr], (g, dp, fr)
         )
 
-    for cc in range(2):
-        far_in(cc).wait_recv()
-        swap_out(cc).start()
-    pow_cp.wait_recv()
+    def weigh(q, j, div):
+        rows, cols = urows(j), slice(q * QW, q * QW + QW)
+        wall[q, dp, rows, :] = ((states[rows, cols] - total[rows, cols]) / div).astype(BF16)
+        for e in (1, 3, 2):
+            wal_out(q, e, j).start()
+        wac_out(q, 0, j).start()
+
     divs = []
-    for j in range(2):
-        power = (pow_s[j : j + 1, :] + pow_r[j : j + 1, :]) / KV + power_eps
-        length = len_row[0:1, pl.ds(pl.multiple_of((mp % 4) * 256 + j * 128, 128), 128)]
-        divs.append(to_col(length * power))
-    for q in range(NQ):
-        for j in range(2):
-            rows = slice(j * 128, (j + 1) * 128)
-            wall[q, dp, rows, :] = (total[rows, q * QW : q * QW + QW] / divs[j]).astype(BF16)
-        for e in (1, 3, 2):
-            wal_out(q, e).start()
-        wac_out(q, 0).start()
+    for j in (1 - g, g):
+        pow_cp(j).wait_recv()
+        power_j = (pow_s[j, 0:1, :] + pow_r[j, 0:1, :]) / KV + power_eps
+        start = pl.multiple_of((mp % 4) * 256 + j * 128, 128)
+        divs.append(to_col(len_row[0:1, pl.ds(start, 128)] * power_j))
+        weigh(0, j, divs[-1])
+    for q in range(1, NQ):
+        for j, div in zip((1 - g, g), divs):
+            weigh(q, j, div)
+    far_in(1 - c).wait_recv()
+    swap_out(1 - c).start()
 
     def accumulate(q, slot):
         grad[q % 2] += jnp.dot(nturn[slot], wall[q, slot], preferred_element_type=F32)
@@ -537,29 +587,27 @@
     def begin(q):
         grad[q % 2] = jnp.zeros((512, QW), F32)
         accumulate(q, dp)
-        wac_in(q, 0).wait_recv()
+        wac_wait(q, 0)
         accumulate(q, x * 2 + 1 - c)
 
     begin(0)
     for q in range(NQ):
         for e in (1, 3):
-            wal_in(q, e).wait_recv()
-            wac_out(q, e).start()
+            pass_on(q, e)
         accumulate(q, xp(-1) * 2 + c)
         accumulate(q, xp(-3) * 2 + c)
         if q == 0:
             for cc in range(2):
                 swap_in(cc).wait_recv()
                 turn(xp(2) * 2 + cc)
-        wal_in(q, 2).wait_recv()
-        wac_out(q, 2).start()
+        pass_on(q, 2)
         accumulate(q, xp(-2) * 2 + c)
         for e in (1, 3):
-            wac_in(q, e).wait_recv()
+            wac_wait(q, e)
             accumulate(q, xp(-e) * 2 + 1 - c)
         if q + 1 < NQ:
             begin(q + 1)
-        wac_in(q, 2).wait_recv()
+        wac_wait(q, 2)
         accumulate(q, xp(-2) * 2 + 1 - c)
         for b in range(16):
             grad_s[q, b] = grad[q % 2, b * 32 : (b + 1) * 32, :].astype(BF16)
@@ -582,7 +630,8 @@
         vc_out(e).wait_send()
     gain_cp.wait_send()
     w_far.wait_send()
-    pow_cp.wait_send()
+    for u in range(2):
+        pow_cp(u).wait_send()
     for i in range(8):
         hid_out[i].wait_send()
         fwd_out[i].wait_send()
@@ -600,15 +649,22 @@
     for e in range(4):
         wc_out(e).wait_send()
         for q in range(NQ):
-            wac_out(q, e).wait_send()
-    nrm_out(x, 1 - c).wait_send()
+            for u in range(2):
+                wac_out(q, e, u).wait_send()
+    nrm_out(x, 1 - c, 0).wait_send()
+    nrm_out(x, 1 - c, 1).wait_send()
     for cc in range(2):
         swap_out(cc).wait_send()
     for e in range(1, 4):
         for q in range(NQ):
-            wal_out(q, e).wait_send()
+            for u in range(2):
+                wal_out(q, e, u).wait_send()
         for cc in range(2):
-            (nrm_out(xp(e), cc) if e != 2 else far_out(cc)).wait_send()
+            if e == 2:
+                far_out(cc).wait_send()
+            else:
+                nrm_out(xp(e), cc, 0).wait_send()
+                nrm_out(xp(e), cc, 1).wait_send()
     for d in range(1, 8):
         sq_out(d).wait_send()
     for q in range(NQ):
@@ -630,9 +686,14 @@
     return pl.pallas_call(
         kernel,
         out_shape=jax.ShapeDtypeStruct((32, 512), F32),
-        in_specs=[pl.BlockSpec(memory_space=pl.ANY)] + [vmem] * 6,
+        in_specs=[pl.BlockSpec(memory_space=pl.ANY)] * 7,
         out_specs=vmem,
         scratch_shapes=[
+            pltpu.VMEM((512,), BF16),
+            pltpu.VMEM((512, 512), BF16),
+            pltpu.VMEM((256, 4096), BF16),
+            pltpu.VMEM((4096,), BF16),
+            pltpu.VMEM((4, 1024), jnp.int32),
             pltpu.VMEM((2048, 512), BF16),
             pltpu.VMEM((2048, 512), BF16),
             pltpu.VMEM((512, 512), BF16),
@@ -647,14 +708,14 @@
             pltpu.VMEM((8, 8, 128), F32),
             pltpu.VMEM((256, 512), F32),
             pltpu.VMEM((256, 512), F32),
-            pltpu.VMEM((8, 128), F32),
-            pltpu.VMEM((8, 128), F32),
+            pltpu.VMEM((2, 8, 128), F32),
+            pltpu.VMEM((2, 8, 128), F32),
             pltpu.VMEM((8, 1024), F32),
             pltpu.VMEM((NQ, 8, 256, QW), BF16),
             pltpu.VMEM((2, 512, QW), F32),
             pltpu.VMEM((NQ, 16, 32, QW), BF16),
             pltpu.VMEM((NQ, 16, 32, QW), BF16),
-            dma((3,)),
+            dma((8,)),
             dma((8,)),
             dma((8,)),
             dma((8,)),
@@ -671,18 +732,20 @@
             dma((3, 2)),
             dma((4,)),
             dma((4,)),
-            dma((8,)),
-            dma((8,)),
+            dma((8, 2)),
+            dma((8, 2)),
+            dma((2,)),
+            dma((2,)),
             dma((2,)),
             dma((2,)),
             dma((2, 4, 2)),
             dma((2, 4, 2)),
             dma((8,)),
             dma((8,)),
-            dma((NQ, 3)),
-            dma((NQ, 3)),
-            dma((NQ, 4)),
-            dma((NQ, 4)),
+            dma((NQ, 3, 2)),
+            dma((NQ, 3, 2)),
+            dma((NQ, 4, 2)),
+            dma((NQ, 4, 2)),
             dma((NQ, 16)),
             dma((NQ, 16)),
         ],

time: 81.3 us -> 79.9 us (0.983)
  Pallas kernels: 78.8 us -> 77.2 us
    pallas_call x1, Pallas kernels: 78.8 us -> 77.2 us  [per_device(): pl.pallas_call(kernel, out_shape=jax.ShapeDtypeStruct((32, 512), F32), in...]
where the time goes in v4:
time: 79.9 us; the launch traced here: 78.7 us
  Pallas kernels  77.2 us (97%)
  local copies, waits for them, and re-layouts  1.47 us (2%)
    pallas_call x1, Pallas kernels, per_device(): pl.pallas_call(kernel, out_shape=jax.ShapeDtypeStruct((32, 512), F32), in...  77.2 us

profile of v4, /device:TPU:8, one launch (start us, length us, event | category | flops | bytes accessed | tf_op | source)
XLA Modules:
  0.0 78.7 jit_solution(13935942350026720969)
XLA Ops:
  0.0 77.2 %shard_map.73 = f32[32,512]{1,0:T(8,128)} custom-call(bf16[4096,512]{1,0:T(8,128)(2,1)} %hid_ref.1, bf16[512]{0:T(512)(128)(2,1)} %gain_in.1, bf16[512,512]{1,0:T(8,128)(2,1)} %val_in.1, bf16[256,4096]{1,0:T(8,128)(2,1)} %stu_in.1, bf16[4096]{0:T(1024)(128)(2,1)} %sgain_in.1, bf16[32,512]{1,0:T(8,128)(2,1)} %wsh_ref.1, s32[4,1024]{1,0:T(4,128)} %seg_in.1), custom_call_target="tpu_custom_call" | custom-call | tf_op jit(solution)/shard_map/pallas_call | solution.py:686
  77.2 1.5 %copy.9 = f32[32,512]{1,0:T(8,128)} copy(f32[32,512]{1,0:T(8,128)} %shard_map.73) | data formatting | bytes 131072

commit v5 on v4

--- a/solution.py
+++ b/solution.py
@@ -685,7 +685,7 @@
     dma = pltpu.SemaphoreType.DMA
     return pl.pallas_call(
         kernel,
-        out_shape=jax.ShapeDtypeStruct((32, 512), F32),
+        out_shape=pltpu.VMEM((32, 512), F32),
         in_specs=[pl.BlockSpec(memory_space=pl.ANY)] * 7,
         out_specs=vmem,
         scratch_shapes=[

time: 79.9 us -> 78.4 us (0.981)
  local copies, waits for them, and re-layouts: 1.47 us -> 0.63 us
    unnamed x1, local copies, waits for them, and re-layouts: 1.47 us -> 0.63 us
where the time goes in v5:
time: 78.4 us; the launch traced here: 77.2 us
  Pallas kernels  76.6 us (98%)
    pallas_call x1, Pallas kernels, per_device(): pl.pallas_call(kernel, out_shape=pltpu.VMEM((32, 512), F32), in_specs=[pl...  76.6 us

profile of v5, /device:TPU:8, one launch (start us, length us, event | category | flops | bytes accessed | tf_op | source)
XLA Modules:
  0.0 77.2 jit_solution(10051422140488058632)
XLA Ops:
  0.0 76.6 %shard_map.73 = f32[32,512]{1,0:T(8,128)S(1)} custom-call(bf16[4096,512]{1,0:T(8,128)(2,1)} %hid_ref.1, bf16[512]{0:T(512)(128)(2,1)} %gain_in.1, bf16[512,512]{1,0:T(8,128)(2,1)} %val_in.1, bf16[256,4096]{1,0:T(8,128)(2,1)} %stu_in.1, bf16[4096]{0:T(1024)(128)(2,1)} %sgain_in.1, bf16[32,512]{1,0:T(8,128)(2,1)} %wsh_ref.1, s32[4,1024]{1,0:T(4,128)} %seg_in.1), custom_call_target="tpu_custom_call" | custom-call | tf_op jit(solution)/shard_map/pallas_call | solution.py:686
  76.6 0.6 copy.9

commit v6 on v5

--- a/solution.py
+++ b/solution.py
@@ -21,6 +21,8 @@
 NQ = 4
 QW = 512 // NQ
 NEAR = (4, 3, -3, 2, -2, 1, -1)
+
+PEERS = [(o, d) for d in NEAR + (0,) for o in (1, 0) if (o, d) != (0, 0)]
 
 
 def kernel(
@@ -549,14 +551,18 @@
             wal_in(q, e, j).wait_recv()
             wac_out(q, e, j).start()
 
+    def peer(t):
+        other, d = PEERS[t]
+        return (1 - h if other else h) * 8 + zp(d)
+
     def grad_out(q, t):
-        to = lax.rem(mp + t, 16)
+        to = peer(t)
         return rc(
             grad_s.at[q, to], grad_r.at[q, mp], grad_ss.at[q, to], grad_rs.at[q, mp], (g, dp, to)
         )
 
     def grad_in(q, t):
-        fr = lax.rem(mp + t, 16)
+        fr = peer(t)
         return rc(
             grad_r.at[q, fr], grad_r.at[q, fr], grad_ss.at[q, fr], grad_rs.at[q, fr], (g, dp, fr)
         )
@@ -611,16 +617,16 @@
         accumulate(q, xp(-2) * 2 + 1 - c)
         for b in range(16):
             grad_s[q, b] = grad[q % 2, b * 32 : (b + 1) * 32, :].astype(BF16)
-        for t in range(1, 16):
+        for t in range(15):
             grad_out(q, t).start()
         out_ref[:, q * QW : q * QW + QW] = grad[q % 2, pl.ds(pl.multiple_of(mp * 32, 32), 32), :]
 
     for q in range(NQ):
-        for t in range(1, 16):
+        for t in range(15):
             grad_in(q, t).wait_recv()
         acc = out_ref[:, q * QW : q * QW + QW]
-        for t in range(1, 16):
-            acc = acc + grad_r[q, lax.rem(mp + t, 16)].astype(F32)
+        for t in range(15):
+            acc = acc + grad_r[q, peer(t)].astype(F32)
         out_ref[:, q * QW : q * QW + QW] = acc
 
     val_cp.wait_send()
@@ -668,7 +674,7 @@
     for d in range(1, 8):
         sq_out(d).wait_send()
     for q in range(NQ):
-        for t in range(1, 16):
+        for t in range(15):
             grad_out(q, t).wait_send()
 
 

time: 78.4 us -> 78.3 us (level)
  no operation moved by 1% of the time
where the time goes in v6:
time: 78.3 us; the launch traced here: 76.8 us
  Pallas kernels  76.2 us (97%)
    pallas_call x1, Pallas kernels, per_device(): pl.pallas_call(kernel, out_shape=pltpu.VMEM((32, 512), F32), in_specs=[pl...  76.2 us

profile of v6, /device:TPU:8, one launch (start us, length us, event | category | flops | bytes accessed | tf_op | source)
XLA Modules:
  0.0 76.8 jit_solution(13267668757429851611)
XLA Ops:
  0.0 76.2 %shard_map.73 = f32[32,512]{1,0:T(8,128)S(1)} custom-call(bf16[4096,512]{1,0:T(8,128)(2,1)} %hid_ref.1, bf16[512]{0:T(512)(128)(2,1)} %gain_in.1, bf16[512,512]{1,0:T(8,128)(2,1)} %val_in.1, bf16[256,4096]{1,0:T(8,128)(2,1)} %stu_in.1, bf16[4096]{0:T(1024)(128)(2,1)} %sgain_in.1, bf16[32,512]{1,0:T(8,128)(2,1)} %wsh_ref.1, s32[4,1024]{1,0:T(4,128)} %seg_in.1), custom_call_target="tpu_custom_call" | custom-call | tf_op jit(solution)/shard_map/pallas_call | solution.py:692
  76.2 0.6 copy.9
